TPU v7x, 512 devices: a whole 4x4x16 slice. The times are simulated.
512 devices in a mesh: bx: 16 (over x_lo, y, core), by: 32 (over z, x_hi).
Axes of the slice: x: 4 (x_hi: 2, x_lo: 2; x = x_hi * 2 + x_lo), y: 4, z: 16, core: 2. Of those that a mesh axis runs over, the one named last changes fastest.
Arguments:
- solution: float32 [4, 2048, 2048], P(None, 'by', 'bx'), may hold values from -6 to 6
- source: float32 [4, 2048, 2048], P(None, 'by', 'bx'), may hold values from -12 to 12
- class_ids: int32 [4, 2048, 2048], P(None, 'by', 'bx'), may hold values from 0 to 7
- conductivity: float32 [8], replicated, may hold values from 0.3 to 3
- spacing_x: float32 [2048], P('bx'), may hold values from 0.7 to 1.4
- spacing_y: float32 [2048], P('by'), may hold values from 0.7 to 1.4
- spacing_z: float32 [4], replicated, may hold values from 0.7 to 1.4
- forward_x: bfloat16 [2048, 2048], P('bx'), may hold values from -0.125 to 0.125
- forward_y: bfloat16 [2048, 2048], P('by'), may hold values from -0.125 to 0.125
- forward_z: bfloat16 [4, 4], replicated, may hold values from -3 to 3
- inverse_x: bfloat16 [2048, 2048], P('bx'), may hold values from -0.125 to 0.125
- inverse_y: bfloat16 [2048, 2048], P('by'), may hold values from -0.125 to 0.125
- inverse_z: bfloat16 [4, 4], replicated, may hold values from -3 to 3
- eigen_x: float32 [2048], P('bx'), may hold values from 0.05 to 4
- eigen_y: float32 [2048], P('by'), may hold values from 0.05 to 4
- eigen_z: float32 [4], replicated, may hold values from 0.05 to 4
Outputs:
- corrected: float32 [4, 2048, 2048], P(None, 'by', 'bx')
All inputs are finite; a program needn't handle non-finite values.
Results may differ from a plain program's by a relative error of at most 0.0039.
Values may be sent and summed in bfloat16 or wider, within the bound.
A program may use at most 64 MiB of HBM per device.

v0:
```python
import jax
import jax.numpy as jnp
from jax import lax
from jax.sharding import Mesh
from jax.sharding import PartitionSpec as P

CLASSES = 8
BY = ("by_0", "by_1")


shift_value = 0.1


def with_halo(value, sides, width):
    edges = {}
    for axis, dim in sides:
        size, length = (lax.axis_size(axis), value.shape[dim])
        up = [(i, (i + 1) % size) for i in range(size - 1)]
        last = lax.slice_in_dim(value, length - width, length, axis=dim)
        first = lax.slice_in_dim(value, 0, width, axis=dim)
        edges[dim] = (
            lax.ppermute(last, axis, up),
            lax.ppermute(first, axis, [(b, a) for a, b in up]),
        )
    done = []
    for _, dim in sides:
        low, high = edges[dim]
        around = [(width, width) if d in done else (0, 0) for d in range(value.ndim)]
        value = jnp.concatenate([jnp.pad(low, around), value, jnp.pad(high, around)], axis=dim)
        done.append(dim)
    return value


def whole_of(value, axes, dim):
    filled = value
    for number in range(len(axes) - 1, -1, -1):
        filled = lax.all_gather(filled, axes[number], axis=dim, tiled=True)
    return filled


def coefficients(class_ids, conductivity):
    result = jnp.zeros(class_ids.shape, jnp.float32)
    for index in range(CLASSES):
        result = result + jnp.where(class_ids == index, conductivity[index], jnp.float32(0.0))
    return result


def operate(solution, coef):
    stacked = jnp.stack([solution, coef])
    padded = with_halo(stacked, (("bx", 3), (BY, 2)), 1)
    padded = jnp.pad(padded, ((0, 0), (1, 1), (0, 0), (0, 0)))
    values = padded[0]
    padcoef = padded[1]
    slices = [
        (slice(2, None), slice(1, -1), slice(1, -1)),
        (slice(0, -2), slice(1, -1), slice(1, -1)),
        (slice(1, -1), slice(2, None), slice(1, -1)),
        (slice(1, -1), slice(0, -2), slice(1, -1)),
        (slice(1, -1), slice(1, -1), slice(2, None)),
        (slice(1, -1), slice(1, -1), slice(0, -2)),
    ]
    result = jnp.zeros(solution.shape, jnp.float32)
    for where_at in slices:
        neighbour = values[where_at]
        ncoef = padcoef[where_at]
        face = jnp.where(ncoef > 0, 2.0 * coef * ncoef / (coef + ncoef), coef)
        result = result + face * (solution - neighbour)
    return result


def x_high(values, matrix_rows):
    columns = matrix_rows.astype(jnp.float32)
    return jnp.einsum(
        "kjx,mx->kjm",
        lax.all_gather(values, "bx", axis=2, tiled=True),
        columns,
        precision=lax.Precision.HIGHEST,
    )


def y_low(values, matrix_rows):
    return jnp.einsum(
        "kjm,nj->knm", whole_of(values, BY, 1), matrix_rows, preferred_element_type=jnp.float32
    )


def on_device(
    solution,
    source,
    class_ids,
    conductivity,
    spacing_x,
    spacing_y,
    spacing_z,
    forward_x,
    forward_y,
    forward_z,
    inverse_x,
    inverse_y,
    inverse_z,
    eigen_x,
    eigen_y,
    eigen_z,
):
    highest = lax.Precision.HIGHEST
    coef = coefficients(class_ids, conductivity)
    operated = operate(solution, coef)
    weights = spacing_z[:, None, None] * spacing_y[None, :, None] * spacing_x[None, None, :]
    restricted = (weights * (source - operated)).astype(jnp.bfloat16)
    modes_xy = x_high(y_low(restricted, forward_y), forward_x)
    modes = jnp.einsum("qk,knm->qnm", forward_z.astype(jnp.float32), modes_xy, precision=highest)
    divisor = eigen_x[None, None, :] + eigen_y[None, :, None] + eigen_z[:, None, None] + shift_value
    scaled = modes / divisor
    spectral = jnp.einsum(
        "kq,qnm->knm", inverse_z.astype(jnp.float32), scaled, precision=highest
    ).astype(jnp.bfloat16)
    field = x_high(y_low(spectral, inverse_y), inverse_x)
    return solution + weights * field


def solution(mesh):
    split = Mesh(mesh.devices.reshape(mesh.shape["bx"], 16, 2), ("bx", "by_0", "by_1"))
    placed = (
        P(None, BY, "bx"),
        P(None, BY, "bx"),
        P(None, BY, "bx"),
        P(),
        P("bx"),
        P(BY),
        P(),
        P("bx", None),
        P(BY, None),
        P(),
        P("bx", None),
        P(BY, None),
        P(),
        P("bx"),
        P(BY),
        P(),
    )
    return jax.shard_map(
        on_device, mesh=split, in_specs=placed, out_specs=P(None, BY, "bx"), check_vma=False
    )
```

profile of v0, /device:TPU:24, one launch (start us, length us, event | category | flops | bytes accessed | tf_op | source)
XLA Modules:
  0.0 304.9 jit_solution(11412667438014760652)
XLA Ops:
  6.5 0.0 copy-start
  6.5 0.0 all-gather.5.cloned.1.call-start
  6.5 1.6 fusion.42
  8.2 0.0 copy-start.1
  8.2 0.0 copy-start.3
  8.2 0.0 copy-start.5
  8.2 0.0 copy-start.6
  8.2 6.0 %fusion.41 = f32[1,4,64,128]{3,2,1,0:T(8,128)S(1)} fusion(f32[]{:T(128)} %bitcast.8, s32[4,64,128]{2,1,0:T(8,128)} %param.18, f32[]{:T(128)} %bitcast.7, f32[]{:T(128)} %bitcast.6, f32[]{:T(128)} %bitcast.5, f32[]{:T(128)} %bitcast.4, f32[]{:T(128)} %bitcast.3, f32[]{:T(128)} %bitcast.2, f32[]{:T(128)} %bitcast.1), kind=kLoop, calls=%fused_computation.69 | loop fusion | flops 753664 | bytes 262176 | tf_op jit(solution)/shard_map/stack | solution.py:49
  14.2 1.1 fusion.14
  15.3 1.9 collective-permute-start.1
  17.2 3.6 %collective-permute-start.2 = (f32[2,4,64,1]{3,2,1,0:T(8,128)S(1)}, f32[2,4,64,1]{3,2,1,0:T(8,128)S(1)}, u32[]{:S(2)}, u32[]{:S(2)}) collective-permute-start(f32[2,4,64,1]{3,2,1,0:T(8,128)S(1)} %get-tuple-element.8), channel_id=1, source_target_pairs={{32,0},{64,32},{96,64},{128,96},{160,128},{192,160},{224,192},{256... | collective-permute-start | bytes 6152 | tf_op jit(solution)/shard_map/ppermute | solution.py:23
  20.9 0.7 pad_maximum_fusion.1
  21.6 4.9 %collective-permute-start = (f32[2,4,1,128]{3,2,1,0:T(1,128)S(1)}, f32[2,4,1,128]{3,2,1,0:T(1,128)S(1)}, u32[]{:S(2)}, u32[]{:S(2)}) collective-permute-start(f32[2,4,1,128]{3,2,1,0:T(1,128)S(1)} %get-tuple-element.9), channel_id=1, source_target_pairs={{0,1},{1,2},{2,3},{3,4},{4,5},{5,6},{6,7},{7,8},{8,9},{9,10},{10,1... | collective-permute-start | bytes 12296 | tf_op jit(solution)/shard_map/ppermute | solution.py:22
  26.6 1.3 collective-permute-start.3
  27.9 0.7 broadcast_multiply_fusion
  28.6 0.0 collective-permute-done.1
  28.6 0.0 collective-permute-done.2
  28.6 0.0 collective-permute-done
  28.6 4.9 %collective-permute-done.3 = f32[2,4,1,128]{3,2,1,0:T(1,128)S(1)} collective-permute-done((f32[2,4,1,128]{3,2,1,0:T(1,128)S(1)}, f32[2,4,1,128]{3,2,1,0:T(1,128)S(1)}, u32[]{:S(2)}, u32[]{:S(2)}) %collective-permute-start.3) | collective-permute-done | bytes 4128 | tf_op jit(solution)/shard_map/ppermute | solution.py:23
  33.6 1.2 select_maximum_fusion
  34.8 0.0 copy-start.4
  34.8 0.1 fusion.11
  34.9 0.0 copy-done.1
  34.9 0.0 copy-done.3
  34.9 0.0 copy-done.5
  34.9 0.0 copy-done.6
  34.9 0.0 copy-start.8
  34.9 0.0 copy-start.9
  34.9 5.5 %fusion.17 = bf16[4,64,128]{2,1,0:T(8,128)(2,1)S(1)} fusion(f32[4,64,128]{2,1,0:T(8,128)S(1)} %copy-done.5, f32[4,64,128]{2,1,0:T(8,128)S(1)} %copy-done.1, f32[6,66,130]{2,1,0:T(8,128)S(1)} %get-tuple-element.6, f32[6,66,130]{2,1,0:T(8,128)S(1)} %get-tuple-element.5, f32[128]{0:T(128)S(1)} %copy-done.6, f32[4,64]{1,0:T(4,128)S(1)} %broadcast_multiply_fusion, ...), kind=kLoop, calls=%fused_computation.30 | loop fusion | flops 2457600 | bytes 2033184 | tf_op jit(solution)/shard_map/convert_element_type | solution.py:109
  40.4 6.5 %all_gather.18 = bf16[4,128,128]{2,1,0:T(8,128)(2,1)} all-gather(bf16[4,64,128]{2,1,0:T(8,128)(2,1)S(1)} %fusion.17), channel_id=1, replica_groups=mesh['bx'=16,'by_0'=16,'by_1'=2] {'by_1'}, dimensions={1}, use_global_device_ids=true | all-gather | bytes 196608 | tf_op jit(solution)/shard_map/all_gather | solution.py:37
  47.0 0.0 all-gather.5.cloned.1.call-update
  47.0 0.0 copy-start.11
  47.0 0.0 copy-start.12
  47.0 0.0 all-gather.7.cloned.1.call-start
  47.1 77.1 %all-gather.5.cloned.1.call-done = bf16[4,2048,128]{2,1,0:T(8,128)(2,1)} async-done(((bf16[4,128,128]{2,1,0:T(8,128)(2,1)}), bf16[4,2048,128]{2,1,0:T(8,128)(2,1)}) %all-gather.5.cloned.1.call-update) | async-done | bytes 2097168 | tf_op jit(solution)/shard_map/all_gather | solution.py:37
  124.2 0.0 copy-done.4
  124.2 2.7 convolution_bitcast_fusion
  126.9 0.0 copy-start.7
  126.9 0.0 all-gather.7.cloned.1.call-update
  126.9 0.0 all-gather.9.cloned.1.call-start
  127.0 0.0 copy-done.8
  127.0 0.0 copy-done.9
  127.0 0.1 broadcast_add_fusion
  127.1 0.0 copy-start.10
  127.1 40.6 %all-gather.7.cloned.1.call-done = f32[4,64,2048]{2,1,0:T(8,128)} async-done(((f32[4,64,128]{2,1,0:T(8,128)}), f32[4,64,2048]{2,1,0:T(8,128)}) %all-gather.7.cloned.1.call-update) | async-done | bytes 2097168 | tf_op jit(solution)/shard_map/all_gather | solution.py:75
  167.7 0.0 copy-done
  167.7 2.7 fusion.9
  170.4 0.0 copy-done.11
  170.4 0.0 copy-done.12
  170.4 0.0 copy-start.2
  170.4 0.3 fusion.6
  170.7 0.0 copy-done.7
  170.7 0.2 fusion.7
  171.0 6.5 %all_gather.21 = bf16[4,128,128]{2,0,1:T(4,128)(2,1)} all-gather(bf16[4,64,128]{2,0,1:T(4,128)(2,1)S(1)} %fusion.7), channel_id=1, replica_groups=mesh['bx'=16,'by_0'=16,'by_1'=2] {'by_1'}, dimensions={1}, use_global_device_ids=true | all-gather | bytes 196608 | tf_op jit(solution)/shard_map/all_gather | solution.py:37
  177.5 0.0 all-gather.9.cloned.1.call-update
  177.6 0.0 all-gather.11.cloned.1.call-start
  177.6 73.9 %all-gather.9.cloned.1.call-done = bf16[4,2048,128]{2,0,1:T(4,128)(2,1)} async-done(((bf16[4,128,128]{2,0,1:T(4,128)(2,1)}), bf16[4,2048,128]{2,0,1:T(4,128)(2,1)}) %all-gather.9.cloned.1.call-update) | async-done | bytes 2097168 | tf_op jit(solution)/shard_map/all_gather | solution.py:37
  251.5 0.0 copy-done.10
  251.5 2.7 fusion.2
  254.2 0.0 all-gather.11.cloned.1.call-update
  254.3 40.8 %all-gather.11.cloned.1.call-done = f32[4,64,2048]{2,1,0:T(8,128)} async-done(((f32[4,64,128]{2,1,0:T(8,128)}), f32[4,64,2048]{2,1,0:T(8,128)}) %all-gather.11.cloned.1.call-update) | async-done | bytes 2097168 | tf_op jit(solution)/shard_map/all_gather | solution.py:75
  295.1 0.0 copy-done.2
  295.1 3.3 %fusion.5 = f32[4,64,128]{2,1,0:T(8,128)} fusion(f32[4,64,128]{2,1,0:T(8,128)S(1)} %copy-done.1, f32[4,64,2048]{2,1,0:T(8,128)} %all-gather.11.cloned.1.call-done, bf16[128,2048]{1,0:T(8,128)(2,1)S(1)} %copy-done.2, f32[128]{0:T(128)S(1)} %copy-done.6, f32[4,64]{1,0:T(4,128)S(1)} %broadcast_multiply_fusion), kind=kOutput, calls=%fused_computation.5 | convolution fusion | flops 805404672 | bytes 2885120 | tf_op jit(solution)/shard_map/kjx,mx->kjm/dot_general | solution.py:73
Async XLA Ops:
  6.5 161.2 %copy-start = (bf16[128,2048]{1,0:T(8,128)(2,1)S(1)}, bf16[128,2048]{1,0:T(8,128)(2,1)}, u32[]{:S(2)}) copy-start(bf16[128,2048]{1,0:T(8,128)(2,1)} %param.23) | copy-start | bytes 1572868
  6.5 117.6 %all-gather.5.cloned.1.call-start = ((), (), s32[]{:S(2)}) async-start(), calls=%async_computation | async-start | bytes 2228224 | tf_op jit(solution)/shard_map/all_gather | solution.py:37
  8.2 26.7 %copy-start.1 = (f32[4,64,128]{2,1,0:T(8,128)S(1)}, f32[4,64,128]{2,1,0:T(8,128)}, u32[]{:S(2)}) copy-start(f32[4,64,128]{2,1,0:T(8,128)} %param.16) | copy-start | bytes 393220
  8.2 26.7 %copy-start.3 = (s32[4,64,128]{2,1,0:T(8,128)S(1)}, s32[4,64,128]{2,1,0:T(8,128)}, u32[]{:S(2)}) copy-start(s32[4,64,128]{2,1,0:T(8,128)} %param.18) | copy-start | bytes 393220
  8.2 26.7 %copy-start.5 = (f32[4,64,128]{2,1,0:T(8,128)S(1)}, f32[4,64,128]{2,1,0:T(8,128)}, u32[]{:S(2)}) copy-start(f32[4,64,128]{2,1,0:T(8,128)} %param.17) | copy-start | bytes 393220
  8.2 26.7 %copy-start.6 = (f32[128]{0:T(128)S(1)}, f32[128]{0:T(128)}, u32[]{:S(2)}) copy-start(f32[128]{0:T(128)} %param.20) | copy-start | bytes 1540
  15.3 13.3 %collective-permute-start.1 = (f32[2,4,64,1]{3,2,1,0:T(8,128)S(1)}, f32[2,4,64,1]{3,2,1,0:T(8,128)S(1)}, u32[]{:S(2)}, u32[]{:S(2)}) collective-permute-start(f32[2,4,64,1]{3,2,1,0:T(8,128)S(1)} %get-tuple-element.7), channel_id=1, source_target_pairs={{0,32},{32,64},{64,96},{96,128},{128,160},{160,192},{192,224},{224... | collective-permute-start | bytes 6152 | tf_op jit(solution)/shard_map/ppermute | solution.py:22
  17.2 11.4 %collective-permute-start.2 = (f32[2,4,64,1]{3,2,1,0:T(8,128)S(1)}, f32[2,4,64,1]{3,2,1,0:T(8,128)S(1)}, u32[]{:S(2)}, u32[]{:S(2)}) collective-permute-start(f32[2,4,64,1]{3,2,1,0:T(8,128)S(1)} %get-tuple-element.8), channel_id=1, source_target_pairs={{32,0},{64,32},{96,64},{128,96},{160,128},{192,160},{224,192},{256... | collective-permute-start | bytes 6152 | tf_op jit(solution)/shard_map/ppermute | solution.py:23
  21.6 7.0 %collective-permute-start = (f32[2,4,1,128]{3,2,1,0:T(1,128)S(1)}, f32[2,4,1,128]{3,2,1,0:T(1,128)S(1)}, u32[]{:S(2)}, u32[]{:S(2)}) collective-permute-start(f32[2,4,1,128]{3,2,1,0:T(1,128)S(1)} %get-tuple-element.9), channel_id=1, source_target_pairs={{0,1},{1,2},{2,3},{3,4},{4,5},{5,6},{6,7},{7,8},{8,9},{9,10},{10,1... | collective-permute-start | bytes 12296 | tf_op jit(solution)/shard_map/ppermute | solution.py:22
  26.6 7.0 %collective-permute-start.3 = (f32[2,4,1,128]{3,2,1,0:T(1,128)S(1)}, f32[2,4,1,128]{3,2,1,0:T(1,128)S(1)}, u32[]{:S(2)}, u32[]{:S(2)}) collective-permute-start(f32[2,4,1,128]{3,2,1,0:T(1,128)S(1)} %get-tuple-element.10), channel_id=1, source_target_pairs={{1,0},{2,1},{3,2},{4,3},{5,4},{6,5},{7,6},{8,7},{9,8},{10,9},{11,1... | collective-permute-start | bytes 12296 | tf_op jit(solution)/shard_map/ppermute | solution.py:23
  34.8 89.4 %copy-start.4 = (bf16[64,2048]{1,0:T(8,128)(2,1)S(1)}, bf16[64,2048]{1,0:T(8,128)(2,1)}, u32[]{:S(2)}) copy-start(bf16[64,2048]{1,0:T(8,128)(2,1)} %param.24) | copy-start | bytes 786436
  34.9 92.0 %copy-start.8 = (f32[64]{0:T(128)S(1)}, f32[64]{0:T(128)}, u32[]{:S(2)}) copy-start(f32[64]{0:T(128)} %param.30) | copy-start | bytes 772
  34.9 92.0 %copy-start.9 = (f32[128]{0:T(128)S(1)}, f32[128]{0:T(128)}, u32[]{:S(2)}) copy-start(f32[128]{0:T(128)} %param.29) | copy-start | bytes 1540
  47.0 123.4 %copy-start.11 = (bf16[4,4]{1,0:T(4,128)(2,1)S(1)}, bf16[4,4]{1,0:T(4,128)(2,1)}, u32[]{:S(2)}) copy-start(bf16[4,4]{1,0:T(4,128)(2,1)} %param.25) | copy-start | bytes 100
  47.0 123.4 %copy-start.12 = (f32[4]{0:T(128)S(1)}, f32[4]{0:T(128)}, u32[]{:S(2)}) copy-start(f32[4]{0:T(128)} %param.31) | copy-start | bytes 52
  47.0 120.7 %all-gather.7.cloned.1.call-start = ((), (), s32[]{:S(2)}) async-start(), calls=%async_computation.1 | async-start | bytes 2228224 | tf_op jit(solution)/shard_map/all_gather | solution.py:75
  126.9 43.9 %copy-start.7 = (bf16[4,4]{1,0:T(4,128)(2,1)S(1)}, bf16[4,4]{1,0:T(4,128)(2,1)}, u32[]{:S(2)}) copy-start(bf16[4,4]{1,0:T(4,128)(2,1)} %param.28) | copy-start | bytes 100
  126.9 124.6 %all-gather.9.cloned.1.call-start = ((), (), s32[]{:S(2)}) async-start(), calls=%async_computation.2 | async-start | bytes 2228224 | tf_op jit(solution)/shard_map/all_gather | solution.py:37
  127.1 124.4 %copy-start.10 = (bf16[64,2048]{1,0:T(8,128)(2,1)S(1)}, bf16[64,2048]{1,0:T(8,128)(2,1)}, u32[]{:S(2)}) copy-start(bf16[64,2048]{1,0:T(8,128)(2,1)} %param.27) | copy-start | bytes 786436
  170.4 124.7 %copy-start.2 = (bf16[128,2048]{1,0:T(8,128)(2,1)S(1)}, bf16[128,2048]{1,0:T(8,128)(2,1)}, u32[]{:S(2)}) copy-start(bf16[128,2048]{1,0:T(8,128)(2,1)} %param.26) | copy-start | bytes 1572868
  177.6 117.5 %all-gather.11.cloned.1.call-start = ((), (), s32[]{:S(2)}) async-start(), calls=%async_computation.3 | async-start | bytes 2228224 | tf_op jit(solution)/shard_map/all_gather | solution.py:75
Sparse Core Ops, SparseCore 0:
  47.1 76.9 all-gather.4
  127.0 40.6 all-gather.6
  177.7 73.7 all-gather.8
  254.4 40.6 all-gather.10
where the time goes:
time: 308 us; the launch traced here: 305 us
  waiting for transfers between devices  237 us (77%)
  other arithmetic  15.4 us (5%)
  between operations  13.4 us (4%)
  blocking collectives  13.1 us (4%)
  matrix products  12 us (4%)
  starting transfers between devices  11.9 us (4%)
    all_gather x2, waiting for transfers between devices, whole_of(): filled = lax.all_gather(filled, axes[number], axis=dim, tiled=True)  151 us
    all_gather x2, waiting for transfers between devices, x_high(): lax.all_gather(values, 'bx', axis=2, tiled=True)  81.5 us
    all_gather x2, blocking collectives, whole_of(): filled = lax.all_gather(filled, axes[number], axis=dim, tiled=True)  13.1 us
    another operation x2, other arithmetic, operate(): stacked = jnp.stack([solution, coef])  7.09 us
    ppermute x2, starting transfers between devices, with_halo(): lax.ppermute(last, axis, up)  6.84 us
  transfers between devices with their start and end apart: 8, of which 5 were waited for; matrix products, arithmetic and copies ran while one was open for 1% of the time, Pallas kernels for 0%

commit v1 on v0

v1 whole, which is shorter than its diff:
```python
import functools

import jax
import jax.numpy as jnp
from jax import lax
from jax.experimental import pallas as pl
from jax.experimental.pallas import tpu as pltpu
from jax.sharding import PartitionSpec as P

CLASSES = 8
SHIFT = 0.1
SUBS = 4
MESH = pl.DeviceIdType.MESH
F32 = jnp.float32
BF16 = jnp.bfloat16


def dot(a, b):
    return lax.dot_general(a, b, (((1,), (0,)), ((), ())), preferred_element_type=F32)


def dot_t(a, b):
    return lax.dot_general(a, b, (((1,), (1,)), ((), ())), preferred_element_type=F32)


def iota(shape, dim):
    return lax.broadcasted_iota(jnp.int32, shape, dim)


def to_row(column, width):
    size = column.shape[0]
    spread = jnp.where(iota((size, width), 0) == iota((size, width), 1), column, 0.0)
    return jnp.sum(spread, axis=0, keepdims=True)


def to_column(row, size):
    width = row.shape[1]
    spread = jnp.where(iota((size, width), 0) == iota((size, width), 1), row, 0.0)
    return jnp.sum(spread, axis=1, keepdims=True)


def face(c, cn):
    return jnp.where(cn > 0, 2.0 * c * cn / (c + cn), c)


def remote(src, dst, send, recv, **where):
    return pltpu.make_async_remote_copy(
        src_ref=src, dst_ref=dst, send_sem=send, recv_sem=recv, device_id=where, device_id_type=MESH
    )


def kernel(
    nbx,
    nby,
    sol_ref,
    src_ref,
    cls_ref,
    cond_ref,
    sx_ref,
    sy_ref,
    sz_ref,
    fx_ref,
    fy_ref,
    fz_ref,
    ix_ref,
    iy_ref,
    iz_ref,
    ex_ref,
    ey_ref,
    ez_ref,
    out_ref,
    coef,
    acc,
    xmsg,
    ymsg,
    xhalo,
    yhalo,
    raw_y,
    keep_y,
    pass_y,
    all_x,
    all_ex,
    pencil,
    half_out,
    half_in,
    tsend,
    tall,
    sall,
    uside,
    halo_send,
    halo_recv,
    load_sem,
    wy_send,
    wy_recv,
    wx_send,
    wx_recv,
    ring_send,
    ring_recv,
    half_send,
    half_recv,
    t_send,
    t_recv,
    s_send,
    s_recv,
    u_send,
    u_recv,
):
    bx, by = lax.axis_index("bx"), lax.axis_index("by")
    nz, nchip = nby // 2, nbx // 2
    z, xh = by // 2, by % 2
    chip, core = bx // 2, bx % 2
    other, sibling = by + 1 - 2 * xh, bx + 1 - 2 * core
    planes, rows, lanes = sol_ref.shape
    sub = rows // SUBS
    quarter = rows // 2

    barrier = pltpu.get_barrier_semaphore()

    def greet(o, _):
        pl.semaphore_signal(
            barrier, inc=1, device_id={"bx": (bx + o) % nbx}, device_id_type=MESH
        )
        return 0

    lax.fori_loop(1, nbx, greet, 0)
    near = (1, nby - 1, 2, nby - 2)
    for step in near:
        pl.semaphore_signal(
            barrier, inc=1, device_id={"by": (by + step) % nby}, device_id_type=MESH
        )

    loads = [
        pltpu.make_async_copy(fy_ref, raw_y.at[0], load_sem.at[0]),
        pltpu.make_async_copy(iy_ref, raw_y.at[1], load_sem.at[1]),
        pltpu.make_async_copy(fx_ref, all_x.at[0, core], load_sem.at[2]),
        pltpu.make_async_copy(ix_ref, all_x.at[1, core], load_sem.at[3]),
    ]
    for load in loads:
        load.start()

    for k in range(planes):
        ids = cls_ref[k]
        value = jnp.zeros(ids.shape, F32)
        for index in range(CLASSES):
            value = jnp.where(ids == index, cond_ref[index], value)
        coef[k] = value
    for which, ref in enumerate((sol_ref, coef)):
        for k in range(planes):
            row = which * planes + k
            v = ref[k]
            xmsg[0, pl.ds(row, 1), :] = to_row(v[:, 0:1], lanes)
            xmsg[1, pl.ds(row, 1), :] = to_row(v[:, lanes - 1 : lanes], lanes)
            ymsg[0, pl.ds(row, 1), :] = v[0:1, :]
            ymsg[1, pl.ds(row, 1), :] = v[rows - 1 : rows, :]

    all_ex[pl.ds(core, 1)] = ex_ref[...].reshape(1, 1, lanes)
    pl.semaphore_wait(barrier, nbx - 1 + len(near))

    halos = [
        remote(xmsg.at[0], xhalo.at[1], halo_send.at[0], halo_recv.at[0], bx=(bx + nbx - 1) % nbx),
        remote(xmsg.at[1], xhalo.at[0], halo_send.at[1], halo_recv.at[1], bx=(bx + 1) % nbx),
        remote(ymsg.at[0], yhalo.at[1], halo_send.at[2], halo_recv.at[2], by=(by + nby - 1) % nby),
        remote(ymsg.at[1], yhalo.at[0], halo_send.at[3], halo_recv.at[3], by=(by + 1) % nby),
    ]
    for copy in halos:
        copy.start()

    shares_x = [
        remote(fx_ref, all_x.at[0, core], wx_send.at[0], wx_recv.at[0], bx=sibling),
        remote(ix_ref, all_x.at[1, core], wx_send.at[1], wx_recv.at[1], bx=sibling),
        remote(all_ex.at[core], all_ex.at[core], wx_send.at[2], wx_recv.at[2], bx=sibling),
    ]
    for copy in shares_x:
        copy.start()

    shares_y = []
    low_lane = iota((rows, 128), 1) < 64
    for which in range(2):
        loads[which].wait()
        for pair in range(raw_y.shape[2] // 256):
            a = raw_y[which, :, 256 * pair : 256 * pair + 128].astype(F32)
            b = raw_y[which, :, 256 * pair + 128 : 256 * pair + 256].astype(F32)
            zero = jnp.where(low_lane, a, pltpu.roll(b, 64, 1))
            one = jnp.where(low_lane, pltpu.roll(a, 64, 1), b)
            where = slice(128 * pair, 128 * pair + 128)
            keep_y[which, pl.ds(xh, 1), :, where] = jnp.where(xh == 0, zero, one).astype(BF16)[None]
            pass_y[which, :, where] = jnp.where(xh == 0, one, zero).astype(BF16)
        copy = remote(
            pass_y.at[which], keep_y.at[which, xh], wy_send.at[which], wy_recv.at[which], by=other
        )
        copy.start()
        shares_y.append(copy)

    row_at, lane_at = iota((rows, lanes), 0), iota((rows, lanes), 1)
    for k in range(planes):
        u, c = sol_ref[k], coef[k]
        total = jnp.zeros((rows, lanes), F32)
        for n in (k + 1, k - 1):
            if 0 <= n < planes:
                total = total + face(c, coef[n]) * (u - sol_ref[n])
            else:
                total = total + c * u
        for dim, at, size in ((0, row_at, rows), (1, lane_at, lanes)):
            for shift, edge in ((1, 0), (size - 1, size - 1)):
                term = face(c, pltpu.roll(c, shift, dim)) * (u - pltpu.roll(u, shift, dim))
                total = total + jnp.where(at == edge, 0.0, term)
        acc[k] = total

    for copy in halos:
        copy.wait_recv()
    sides = (bx == 0, bx == nbx - 1, by == 0, by == nby - 1)
    ycol = to_column(sy_ref[...].reshape(1, rows), rows)
    area = ycol * sx_ref[...].reshape(1, lanes)
    for k in range(planes):
        u, c = sol_ref[k], coef[k]
        un, cn = [], []
        for side in range(2):
            halo = xhalo[side]
            gone = sides[side]
            un.append(jnp.where(gone, 0.0, to_column(halo[k : k + 1, :], rows)))
            cn.append(jnp.where(gone, 0.0, to_column(halo[planes + k : planes + k + 1, :], rows)))
        left = lane_at == 0
        term = face(c, jnp.where(left, cn[0], cn[1])) * (u - jnp.where(left, un[0], un[1]))
        total = acc[k] + jnp.where(left | (lane_at == lanes - 1), term, 0.0)
        for side, edge in ((0, 0), (1, rows - 1)):
            halo = yhalo[side]
            gone = sides[2 + side]
            un1 = jnp.where(gone, 0.0, halo[k : k + 1, :])
            cn1 = jnp.where(gone, 0.0, halo[planes + k : planes + k + 1, :])
            term = face(c, cn1) * (u - un1)
            total = total + jnp.where(row_at == edge, term, 0.0)
        value = (sz_ref[k] * area) * (src_ref[k] - total)
        at = pl.ds(pl.multiple_of(z * rows, rows), rows)
        pencil[0, at, k * lanes : (k + 1) * lanes] = value.astype(BF16)

    half = nz // 2

    def ring(phase):
        def hop(direction, d, s):
            sign = 1 - 2 * direction
            plane = (z - sign * d + 2 * nz) % nz
            part = (s + 2 * core) % SUBS
            at = pl.ds(pl.multiple_of(plane * rows + part * sub, sub), sub)
            view = pencil.at[phase, at, :]
            return remote(
                view,
                view,
                ring_send.at[phase, direction, d, s],
                ring_recv.at[phase, direction, d, s],
                by=(by + 2 * sign + nby) % nby,
            )

        def last(direction, s):
            return (s < SUBS // 2) == (direction == 0)

        for s in range(SUBS):
            for direction in range(2):
                hop(direction, 0, s).start()

        def step(d, _):
            for s in range(SUBS):
                for direction in range(2):
                    hop(direction, d - 1, s).wait_recv()
                    hop(direction, d, s).start()
            return 0

        lax.fori_loop(1, half - 1, step, 0)
        for s in range(SUBS):
            for direction in range(2):
                hop(direction, half - 2, s).wait_recv()
                if last(direction, s):
                    hop(direction, half - 1, s).start()
        for s in range(SUBS):
            for direction in range(2):
                if last(direction, s):
                    hop(direction, half - 1, s).wait_recv()

        def finish(d, _):
            for s in range(SUBS):
                for direction in range(2):
                    hop(direction, d, s).wait_send()
            return 0

        lax.fori_loop(0, half - 1, finish, 0)
        for s in range(SUBS):
            for direction in range(2):
                if last(direction, s):
                    hop(direction, half - 1, s).wait_send()

    def contract_y(phase):
        shares_y[phase].wait_recv()
        width = pencil.shape[2] // 2
        mine, copies = [], []
        for piece in range(2):
            at = slice(piece * width, (piece + 1) * width)
            whole = pencil[phase, :, at]
            gone = dot(keep_y[phase, 1 - xh], whole)
            half_out[phase, piece] = gone.astype(BF16)
            copy = remote(
                half_out.at[phase, piece],
                half_in.at[phase, piece],
                half_send.at[phase, piece],
                half_recv.at[phase, piece],
                by=other,
            )
            copy.start()
            copies.append(copy)
            mine.append(dot(keep_y[phase, xh], whole))
        for piece in range(2):
            copies[piece].wait_recv()
            mine[piece] = mine[piece] + half_in[phase, piece].astype(F32)
        for copy in copies:
            copy.wait_send()
        return [
            mine[k // (planes // 2)][:, (k % (planes // 2)) * lanes : (k % (planes // 2) + 1) * lanes]
            for k in range(planes)
        ]

    ring(0)
    modes_y = contract_y(0)

    for k in range(planes):
        for side in range(2):
            tsend[side, k * quarter : (k + 1) * quarter, :] = modes_y[k][
                side * quarter : (side + 1) * quarter, :
            ].astype(BF16)

    def t_copy(o):
        to = (bx + o) % nbx
        return remote(tsend.at[to % 2], tall.at[bx], t_send.at[o], t_recv.at[o], bx=to)

    def start_t(o, _):
        t_copy(o).start()
        return 0

    lax.fori_loop(1, nbx, start_t, 0)
    tall[pl.ds(bx, 1)] = tsend[pl.ds(core, 1)]
    for load in loads[2:]:
        load.wait()
    for copy in shares_x:
        copy.wait_recv()

    def wait_t(o, _):
        t_copy(o).wait_recv()
        return 0

    lax.fori_loop(1, nbx, wait_t, 0)
    rows_x = jnp.concatenate([tall[n] for n in range(nbx)], axis=1)
    half_modes = dot_t(rows_x, all_x[0].reshape(2 * lanes, all_x.shape[3]))

    planes_xy = [half_modes[k * quarter : (k + 1) * quarter, :] for k in range(planes)]
    ey = to_column(ey_ref[...].reshape(1, rows), rows)
    ey = jnp.where(core == 0, ey[:quarter], ey[quarter:])
    ex = jnp.concatenate([all_ex[0], all_ex[1]], axis=1)
    fz, iz = fz_ref[...].astype(F32), iz_ref[...].astype(F32)
    scaled = []
    for q in range(planes):
        mode = sum(fz[q : q + 1, k : k + 1] * planes_xy[k] for k in range(planes))
        scaled.append(mode / (ex + ey + ez_ref[q] + SHIFT))
    for k in range(planes):
        value = sum(iz[k : k + 1, q : q + 1] * scaled[q] for q in range(planes))
        sall[pl.ds(chip, 1), k * quarter : (k + 1) * quarter, :] = value.astype(BF16)[None]

    def s_copy(o):
        to = (chip + o) % nchip
        return remote(
            sall.at[chip], sall.at[chip], s_send.at[o], s_recv.at[o], bx=to * 2 + core
        )

    def start_s(o, _):
        s_copy(o).start()
        return 0

    def wait_s(o, _):
        s_copy(o).wait_recv()
        return 0

    lax.fori_loop(1, nchip, start_s, 0)
    lax.fori_loop(1, nchip, wait_s, 0)
    rows_m = jnp.concatenate([sall[n] for n in range(nchip)], axis=1)
    cells_x = dot_t(rows_m, all_x[1].reshape(2 * lanes, all_x.shape[3])).astype(BF16)

    at = pl.ds(pl.multiple_of(z * rows + core * quarter, quarter), quarter)
    for k in range(planes):
        piece = cells_x[k * quarter : (k + 1) * quarter, :]
        low, high = piece[:, :lanes], piece[:, lanes:]
        pencil[1, at, k * lanes : (k + 1) * lanes] = jnp.where(core == 0, low, high)
        uside[:, k * lanes : (k + 1) * lanes] = jnp.where(core == 0, high, low)
    copy = remote(uside, pencil.at[1, at, :], u_send.at[0], u_recv.at[0], bx=sibling)
    copy.start()
    copy.wait()

    ring(1)
    field = contract_y(1)
    for k in range(planes):
        out_ref[k] = sol_ref[k] + (sz_ref[k] * area) * field[k]

    for copy in halos + shares_x + shares_y:
        copy.wait_send()

    def end_t(o, _):
        t_copy(o).wait_send()
        return 0

    def end_s(o, _):
        s_copy(o).wait_send()
        return 0

    lax.fori_loop(1, nbx, end_t, 0)
    lax.fori_loop(1, nchip, end_s, 0)


def on_device(nbx, nby, *args):
    sol, forward_x, forward_y = args[0], args[7], args[8]
    planes, rows, lanes = sol.shape
    nx, ny = forward_x.shape[1], forward_y.shape[1]
    half = nby // 4
    quarter = rows // 2
    wide = planes * lanes
    vmem = pl.BlockSpec(memory_space=pltpu.VMEM)
    smem = pl.BlockSpec(memory_space=pltpu.SMEM)
    away = pl.BlockSpec(memory_space=pl.ANY)
    dma = pltpu.SemaphoreType.DMA
    specs = [vmem, vmem, vmem, smem, vmem, vmem, smem, away, away, vmem, away, away, vmem, vmem, vmem, smem]
    return pl.pallas_call(
        functools.partial(kernel, nbx, nby),
        out_shape=jax.ShapeDtypeStruct(sol.shape, F32),
        in_specs=specs,
        out_specs=vmem,
        scratch_shapes=[
            pltpu.VMEM((planes, rows, lanes), F32),
            pltpu.VMEM((planes, rows, lanes), F32),
            pltpu.VMEM((2, 2 * planes, lanes), F32),
            pltpu.VMEM((2, 2 * planes, lanes), F32),
            pltpu.VMEM((2, 2 * planes, lanes), F32),
            pltpu.VMEM((2, 2 * planes, lanes), F32),
            pltpu.VMEM((2, rows, ny), BF16),
            pltpu.VMEM((2, 2, rows, ny // 2), BF16),
            pltpu.VMEM((2, rows, ny // 2), BF16),
            pltpu.VMEM((2, 2, lanes, nx), BF16),
            pltpu.VMEM((2, 1, lanes), F32),
            pltpu.VMEM((2, ny // 2, wide), BF16),
            pltpu.VMEM((2, 2, rows, wide // 2), BF16),
            pltpu.VMEM((2, 2, rows, wide // 2), BF16),
            pltpu.VMEM((2, planes * quarter, lanes), BF16),
            pltpu.VMEM((nbx, planes * quarter, lanes), BF16),
            pltpu.VMEM((nbx // 2, planes * quarter, 2 * lanes), BF16),
            pltpu.VMEM((quarter, wide), BF16),
            dma((4,)),
            dma((4,)),
            dma((4,)),
            dma((2,)),
            dma((2,)),
            dma((3,)),
            dma((3,)),
            dma((2, 2, half, SUBS)),
            dma((2, 2, half, SUBS)),
            dma((2, 2)),
            dma((2, 2)),
            dma((nbx,)),
            dma((nbx,)),
            dma((nbx // 2,)),
            dma((nbx // 2,)),
            dma((1,)),
            dma((1,)),
        ],
        compiler_params=pltpu.CompilerParams(
            collective_id=0, has_side_effects=True, vmem_limit_bytes=40 << 20
        ),
    )(*args)


def solution(mesh):
    nbx, nby = mesh.shape["bx"], mesh.shape["by"]
    brick = P(None, "by", "bx")
    placed = (
        brick, brick, brick, P(), P("bx"), P("by"), P(), P("bx", None), P("by", None), P(),
        P("bx", None), P("by", None), P(), P("bx"), P("by"), P(),
    )
    return jax.shard_map(
        functools.partial(on_device, nbx, nby),
        mesh=mesh,
        in_specs=placed,
        out_specs=brick,
        check_vma=False,
    )
```

time: 308 us -> 114 us (0.37)
  waiting for transfers between devices: 237 us -> 0 us
  Pallas kernels: 0 us -> 99.8 us
  other arithmetic: 15.4 us -> 0 us
  between operations: 13.4 us -> 0.03 us
  blocking collectives: 13.1 us -> 0 us
  matrix products: 12 us -> 0 us
  starting transfers between devices: 11.9 us -> 0 us
  local copies, waits for them, and re-layouts: 1.75 us -> 13.3 us
    all_gather x4 -> x0, waiting for transfers between devices: 232 us -> none  [the longest x2 151 us: whole_of(): filled = lax.all_gather(filled, axes[number], axis=dim, tiled=True)]
    pallas_call x0 -> x1, Pallas kernels: none -> 99.8 us  [on_device(): pl.pallas_call(functools.partial(kernel, nbx, nby), out_shape=jax.ShapeDt...]
    unnamed x26 -> x33, local copies, waits for them, and re-layouts: 0.07 us -> 13.3 us
    all_gather x2 -> x0, blocking collectives: 13.1 us -> none  [whole_of(): filled = lax.all_gather(filled, axes[number], axis=dim, tiled=True)]
    dot_general x6 -> x0, matrix products: 12 us -> none  [the longest x2 5.99 us: x_high(): jnp.einsum('kjx,mx->kjm', lax.all_gather(values, 'bx', axis=2, tiled=True...]
    ppermute x4 -> x0, starting transfers between devices: 11.8 us -> none  [the longest x2 6.84 us: with_halo(): lax.ppermute(last, axis, up)]
    another operation x2 -> x0, other arithmetic: 7.09 us -> none  [operate(): stacked = jnp.stack([solution, coef])]
    convert_element_type x1 -> x0, other arithmetic: 5.47 us -> none  [on_device(): restricted = (weights * (source - operated)).astype(jnp.bfloat16)]
  transfers between devices with their start and end apart: 8 -> 0, of which waited for: 5 -> 0; matrix products, arithmetic and copies ran while one was open for 1% -> 0% of each run, Pallas kernels for 0% -> 0%
where the time goes in v1:
time: 114 us; the launch traced here: 113 us
  Pallas kernels  99.8 us (88%)
  local copies, waits for them, and re-layouts  13.3 us (12%)
    pallas_call x1, Pallas kernels, on_device(): pl.pallas_call(functools.partial(kernel, nbx, nby), out_shape=jax.ShapeDt...  99.8 us
    unnamed x33, local copies, waits for them, and re-layouts  13.3 us

profile of v1, /device:TPU:24, one launch (start us, length us, event | category | flops | bytes accessed | tf_op | source)
XLA Modules:
  0.0 113.1 jit_solution(11877180942946888643)
XLA Ops:
  0.0 0.0 copy-start
  0.0 1.0 copy-done
  1.0 0.0 copy-start.1
  1.0 1.0 copy-done.1
  2.1 0.0 copy-start.2
  2.1 0.9 copy-done.2
  3.0 0.0 copy-start.3
  3.0 0.9 copy-done.3
  4.0 0.0 copy-start.4
  4.0 0.9 copy-done.4
  4.9 0.0 copy-start.5
  4.9 0.9 copy-done.5
  5.8 0.0 copy-start.6
  5.8 0.9 copy-done.6
  6.7 0.0 copy-start.7
  6.7 0.7 copy-done.7
  7.4 0.0 copy-start.8
  7.4 0.7 copy-done.8
  8.1 0.0 copy-start.9
  8.1 0.7 copy-done.9
  8.7 0.0 copy-start.10
  8.7 0.7 copy-done.10
  9.4 0.0 copy-start.11
  9.4 0.7 copy-done.11
  10.0 0.0 copy-start.12
  10.0 0.7 copy-done.12
  10.7 0.0 copy-start.13
  10.7 0.7 copy-done.13
  11.3 0.0 copy-start.14
  11.3 0.7 copy-done.14
  12.0 0.0 copy-start.15
  12.0 0.7 copy-done.15
  12.6 99.8 %shard_map.154 = f32[4,64,128]{2,1,0:T(8,128)S(1)} custom-call(f32[4,64,128]{2,1,0:T(8,128)S(1)} %copy-done.4, f32[4,64,128]{2,1,0:T(8,128)S(1)} %copy-done.5, s32[4,64,128]{2,1,0:T(8,128)S(1)} %copy-done.6, f32[8]{0:T(128)S(1)} %copy-done.9, f32[128]{0:T(128)S(1)} %copy-done.10, f32[64]{0:T(128)S(1)} %copy-done.11, f32[4]{0:T(128)S(1)} %copy-done.12, ...), custom_call_target="tpu_custom_call" | custom-call | tf_op jit(solution)/shard_map/pallas_call | solution.py:425
  112.5 0.7 copy.18
Async XLA Ops:
  0.0 1.0 copy-start
  1.0 1.0 copy-start.1
  2.1 0.9 copy-start.2
  3.0 0.9 copy-start.3
  4.0 0.9 copy-start.4
  4.9 0.9 copy-start.5
  5.8 0.9 copy-start.6
  6.7 0.7 copy-start.7
  7.4 0.7 copy-start.8
  8.1 0.7 copy-start.9
  8.7 0.7 copy-start.10
  9.4 0.7 copy-start.11
  10.0 0.7 copy-start.12
  10.7 0.7 copy-start.13
  11.3 0.7 copy-start.14
  12.0 0.7 copy-start.15

commit v2 on v1

--- a/solution.py
+++ b/solution.py
@@ -52,6 +52,23 @@
 def kernel(
     nbx,
     nby,
+    sol_far,
+    src_far,
+    cls_far,
+    cond_far,
+    sx_far,
+    sy_far,
+    sz_far,
+    fx_ref,
+    fy_ref,
+    fz_far,
+    ix_ref,
+    iy_ref,
+    iz_far,
+    ex_far,
+    ey_far,
+    ez_far,
+    out_ref,
     sol_ref,
     src_ref,
     cls_ref,
@@ -59,16 +76,12 @@
     sx_ref,
     sy_ref,
     sz_ref,
-    fx_ref,
-    fy_ref,
     fz_ref,
-    ix_ref,
-    iy_ref,
     iz_ref,
     ex_ref,
     ey_ref,
     ez_ref,
-    out_ref,
+    small_sem,
     coef,
     acc,
     xmsg,
@@ -123,12 +136,33 @@
         return 0
 
     lax.fori_loop(1, nbx, greet, 0)
-    near = (1, nby - 1, 2, nby - 2)
+    near = (1, nby - 1, 2, nby - 2, 4, nby - 4, 6, nby - 6)
     for step in near:
         pl.semaphore_signal(
             barrier, inc=1, device_id={"by": (by + step) % nby}, device_id_type=MESH
         )
 
+    smalls = [
+        pltpu.make_async_copy(far, ref, small_sem.at[n])
+        for n, (far, ref) in enumerate(
+            (
+                (cls_far, cls_ref),
+                (cond_far, cond_ref),
+                (sol_far, sol_ref),
+                (ex_far, ex_ref),
+                (src_far, src_ref),
+                (sx_far, sx_ref),
+                (sy_far, sy_ref),
+                (sz_far, sz_ref),
+                (fz_far, fz_ref),
+                (iz_far, iz_ref),
+                (ey_far, ey_ref),
+                (ez_far, ez_ref),
+            )
+        )
+    ]
+    for load in smalls:
+        load.start()
     loads = [
         pltpu.make_async_copy(fy_ref, raw_y.at[0], load_sem.at[0]),
         pltpu.make_async_copy(iy_ref, raw_y.at[1], load_sem.at[1]),
@@ -138,6 +172,8 @@
     for load in loads:
         load.start()
 
+    for load in smalls[:4]:
+        load.wait()
     for k in range(planes):
         ids = cls_ref[k]
         value = jnp.zeros(ids.shape, F32)
@@ -206,6 +242,8 @@
                 total = total + jnp.where(at == edge, 0.0, term)
         acc[k] = total
 
+    for load in smalls[4:]:
+        load.wait()
     for copy in halos:
         copy.wait_recv()
     sides = (bx == 0, bx == nbx - 1, by == 0, by == nby - 1)
@@ -233,59 +271,55 @@
         at = pl.ds(pl.multiple_of(z * rows, rows), rows)
         pencil[0, at, k * lanes : (k + 1) * lanes] = value.astype(BF16)
 
-    half = nz // 2
-
     def ring(phase):
-        def hop(direction, d, s):
-            sign = 1 - 2 * direction
-            plane = (z - sign * d + 2 * nz) % nz
+        def hop(number, behind, ahead, s):
+            plane = (z - behind + 2 * nz) % nz
             part = (s + 2 * core) % SUBS
             at = pl.ds(pl.multiple_of(plane * rows + part * sub, sub), sub)
             view = pencil.at[phase, at, :]
             return remote(
                 view,
                 view,
-                ring_send.at[phase, direction, d, s],
-                ring_recv.at[phase, direction, d, s],
-                by=(by + 2 * sign + nby) % nby,
+                ring_send.at[phase, number, s],
+                ring_recv.at[phase, (behind + ahead) % nz, s],
+                by=(by + 2 * ahead + nby) % nby,
             )
 
-        def last(direction, s):
-            return (s < SUBS // 2) == (direction == 0)
-
-        for s in range(SUBS):
-            for direction in range(2):
-                hop(direction, 0, s).start()
-
-        def step(d, _):
-            for s in range(SUBS):
-                for direction in range(2):
-                    hop(direction, d - 1, s).wait_recv()
-                    hop(direction, d, s).start()
+        def arrive(behind, s):
+            hop(0, behind, 0, s).wait_recv()
+
+        parts = range(SUBS)
+        for s in parts:
+            for number, ahead in enumerate((3, -3)):
+                hop(number, 0, ahead, s).start()
+        for s in parts:
+            for number, ahead in enumerate((1, -1)):
+                hop(2 + number, 0, ahead, s).start()
+        for s in parts:
+            for side, sign in enumerate((1, -1)):
+                arrive(3 * sign, s)
+                for number, ahead in enumerate((3 * sign, sign, -sign)):
+                    hop(4 + 3 * side + number, 3 * sign, ahead, s).start()
+        for s in parts:
+            for side, sign in enumerate((1, -1)):
+                arrive(6 * sign, s)
+                for number, ahead in enumerate((sign, -sign)):
+                    hop(10 + 2 * side + number, 6 * sign, ahead, s).start()
+                if (s < SUBS // 2) == (side == 0):
+                    hop(14, 6 * sign, 2 * sign, s).start()
+        for behind in (1, 2, 4, 5, 7):
+            for s in parts:
+                for sign in (1, -1):
+                    arrive(behind * sign, s)
+        for s in parts:
+            arrive(8, s)
+
+        def finish(number, _):
+            for s in parts:
+                hop(number, 0, 1, s).wait_send()
             return 0
 
-        lax.fori_loop(1, half - 1, step, 0)
-        for s in range(SUBS):
-            for direction in range(2):
-                hop(direction, half - 2, s).wait_recv()
-                if last(direction, s):
-                    hop(direction, half - 1, s).start()
-        for s in range(SUBS):
-            for direction in range(2):
-                if last(direction, s):
-                    hop(direction, half - 1, s).wait_recv()
-
-        def finish(d, _):
-            for s in range(SUBS):
-                for direction in range(2):
-                    hop(direction, d, s).wait_send()
-            return 0
-
-        lax.fori_loop(0, half - 1, finish, 0)
-        for s in range(SUBS):
-            for direction in range(2):
-                if last(direction, s):
-                    hop(direction, half - 1, s).wait_send()
+        lax.fori_loop(0, 15, finish, 0)
 
     def contract_y(phase):
         shares_y[phase].wait_recv()
@@ -411,23 +445,24 @@
 
 
 def on_device(nbx, nby, *args):
-    sol, forward_x, forward_y = args[0], args[7], args[8]
+    sol, forward_x = args[0], args[7]
     planes, rows, lanes = sol.shape
-    nx, ny = forward_x.shape[1], forward_y.shape[1]
-    half = nby // 4
+    nx, ny = forward_x.shape[1], rows * nby
     quarter = rows // 2
     wide = planes * lanes
     vmem = pl.BlockSpec(memory_space=pltpu.VMEM)
-    smem = pl.BlockSpec(memory_space=pltpu.SMEM)
-    away = pl.BlockSpec(memory_space=pl.ANY)
+    far = pl.BlockSpec(memory_space=pltpu.HBM)
     dma = pltpu.SemaphoreType.DMA
-    specs = [vmem, vmem, vmem, smem, vmem, vmem, smem, away, away, vmem, away, away, vmem, vmem, vmem, smem]
+    near = [pltpu.VMEM] * 3 + [pltpu.SMEM] + [pltpu.VMEM] * 2 + [pltpu.SMEM]
+    near += [None] * 2 + [pltpu.VMEM] + [None] * 2 + [pltpu.VMEM] * 3 + [pltpu.SMEM]
     return pl.pallas_call(
         functools.partial(kernel, nbx, nby),
         out_shape=jax.ShapeDtypeStruct(sol.shape, F32),
-        in_specs=specs,
+        in_specs=[far] * len(args),
         out_specs=vmem,
-        scratch_shapes=[
+        scratch_shapes=[space(arg.shape, arg.dtype) for space, arg in zip(near, args) if space]
+        + [
+            dma((12,)),
             pltpu.VMEM((planes, rows, lanes), F32),
             pltpu.VMEM((planes, rows, lanes), F32),
             pltpu.VMEM((2, 2 * planes, lanes), F32),
@@ -453,8 +488,8 @@
             dma((2,)),
             dma((3,)),
             dma((3,)),
-            dma((2, 2, half, SUBS)),
-            dma((2, 2, half, SUBS)),
+            dma((2, nby // 2 - 1, SUBS)),
+            dma((2, nby // 2, SUBS)),
             dma((2, 2)),
             dma((2, 2)),
             dma((nbx,)),
@@ -465,7 +500,7 @@
             dma((1,)),
         ],
         compiler_params=pltpu.CompilerParams(
-            collective_id=0, has_side_effects=True, vmem_limit_bytes=40 << 20
+            collective_id=0, has_side_effects=True, vmem_limit_bytes=60 << 20
         ),
     )(*args)
 

time: 114 us -> 89.3 us (0.78)
  Pallas kernels: 99.8 us -> 87.4 us
  local copies, waits for them, and re-layouts: 13.3 us -> 1.57 us
    pallas_call x1, Pallas kernels: 99.8 us -> 87.4 us  [on_device(): pl.pallas_call(functools.partial(kernel, nbx, nby), out_shape=jax.ShapeDt...]
    unnamed x33 -> x1, local copies, waits for them, and re-layouts: 13.3 us -> 1.57 us
where the time goes in v2:
time: 89.3 us; the launch traced here: 89 us
  Pallas kernels  87.4 us (98%)
  local copies, waits for them, and re-layouts  1.57 us (2%)
    pallas_call x1, Pallas kernels, on_device(): pl.pallas_call(functools.partial(kernel, nbx, nby), out_shape=jax.ShapeDt...  87.4 us

profile of v2, /device:TPU:24, one launch (start us, length us, event | category | flops | bytes accessed | tf_op | source)
XLA Modules:
  0.0 89.0 jit_solution(5649637741239923534)
XLA Ops:
  0.0 87.4 %shard_map.154 = f32[4,64,128]{2,1,0:T(8,128)} custom-call(f32[4,64,128]{2,1,0:T(8,128)} %sol_far.1, f32[4,64,128]{2,1,0:T(8,128)} %src_far.1, s32[4,64,128]{2,1,0:T(8,128)} %cls_far.1, f32[8]{0:T(128)} %cond_far.1, f32[128]{0:T(128)} %sx_far.1, f32[64]{0:T(128)} %sy_far.1, f32[4]{0:T(128)} %sz_far.1, bf16[128,2048]{1,0:T(8,128)(2,1)} %fx_ref.1, ...), custom_call_target="tpu_custom_call" | custom-call | tf_op jit(solution)/shard_map/pallas_call | solution.py:458
  87.4 1.6 %copy.18 = f32[4,64,128]{2,1,0:T(8,128)} copy(f32[4,64,128]{2,1,0:T(8,128)} %shard_map.154) | data formatting | bytes 262144

commit v3 on v2

--- a/solution.py
+++ b/solution.py
@@ -9,7 +9,7 @@
 
 CLASSES = 8
 SHIFT = 0.1
-SUBS = 4
+SUBS = 2
 MESH = pl.DeviceIdType.MESH
 F32 = jnp.float32
 BF16 = jnp.bfloat16
@@ -119,19 +119,29 @@
     u_recv,
 ):
     bx, by = lax.axis_index("bx"), lax.axis_index("by")
-    nz, nchip = nby // 2, nbx // 2
+    nz, ny4 = nby // 2, nbx // 4
     z, xh = by // 2, by % 2
-    chip, core = bx // 2, bx % 2
-    other, sibling = by + 1 - 2 * xh, bx + 1 - 2 * core
+    xl, row4, core = bx // (2 * ny4), (bx // 2) % ny4, bx % 2
+    mine4 = 2 * xl + core
+    other = by + 1 - 2 * xh
+
+    def relative(j):
+        xl2 = xl if j < 2 else 1 - xl
+        core2 = core if j % 2 == 0 else 1 - core
+        return (xl2 * ny4 + row4) * 2 + core2, 2 * xl2 + core2
+
     planes, rows, lanes = sol_ref.shape
     sub = rows // SUBS
-    quarter = rows // 2
+    quarter = rows // 4
 
     barrier = pltpu.get_barrier_semaphore()
 
     def greet(o, _):
         pl.semaphore_signal(
             barrier, inc=1, device_id={"bx": (bx + o) % nbx}, device_id_type=MESH
+        )
+        pl.semaphore_signal(
+            barrier, inc=1, device_id={"bx": (bx + o) % nbx, "by": other}, device_id_type=MESH
         )
         return 0
 
@@ -166,8 +176,8 @@
     loads = [
         pltpu.make_async_copy(fy_ref, raw_y.at[0], load_sem.at[0]),
         pltpu.make_async_copy(iy_ref, raw_y.at[1], load_sem.at[1]),
-        pltpu.make_async_copy(fx_ref, all_x.at[0, core], load_sem.at[2]),
-        pltpu.make_async_copy(ix_ref, all_x.at[1, core], load_sem.at[3]),
+        pltpu.make_async_copy(fx_ref, all_x.at[0, mine4], load_sem.at[2]),
+        pltpu.make_async_copy(ix_ref, all_x.at[1, mine4], load_sem.at[3]),
     ]
     for load in loads:
         load.start()
@@ -189,8 +199,8 @@
             ymsg[0, pl.ds(row, 1), :] = v[0:1, :]
             ymsg[1, pl.ds(row, 1), :] = v[rows - 1 : rows, :]
 
-    all_ex[pl.ds(core, 1)] = ex_ref[...].reshape(1, 1, lanes)
-    pl.semaphore_wait(barrier, nbx - 1 + len(near))
+    all_ex[pl.ds(mine4, 1)] = ex_ref[...].reshape(1, 1, lanes)
+    pl.semaphore_wait(barrier, 2 * (nbx - 1) + len(near))
 
     halos = [
         remote(xmsg.at[0], xhalo.at[1], halo_send.at[0], halo_recv.at[0], bx=(bx + nbx - 1) % nbx),
@@ -199,14 +209,6 @@
         remote(ymsg.at[1], yhalo.at[0], halo_send.at[3], halo_recv.at[3], by=(by + 1) % nby),
     ]
     for copy in halos:
-        copy.start()
-
-    shares_x = [
-        remote(fx_ref, all_x.at[0, core], wx_send.at[0], wx_recv.at[0], bx=sibling),
-        remote(ix_ref, all_x.at[1, core], wx_send.at[1], wx_recv.at[1], bx=sibling),
-        remote(all_ex.at[core], all_ex.at[core], wx_send.at[2], wx_recv.at[2], bx=sibling),
-    ]
-    for copy in shares_x:
         copy.start()
 
     shares_y = []
@@ -246,6 +248,24 @@
         load.wait()
     for copy in halos:
         copy.wait_recv()
+
+    shares_x = []
+    for which, ref in enumerate((fx_ref, ix_ref)):
+        for j in (1, 2):
+            at, number = all_x.at[which, mine4], 3 * which + j - 1
+            shares_x.append(
+                remote(ref, at, wx_send.at[number], wx_recv.at[number], bx=relative(j)[0])
+            )
+    for j in (1, 2, 3):
+        at, number = all_ex.at[mine4], 5 + j
+        shares_x.append(remote(at, at, wx_send.at[number], wx_recv.at[number], bx=relative(j)[0]))
+    for copy in shares_x[4:] + shares_x[:4]:
+        copy.start()
+
+    def pass_x(which):
+        at, number = all_x.at[which, relative(2)[1]], 3 * which + 2
+        return remote(at, at, wx_send.at[number], wx_recv.at[number], bx=relative(1)[0])
+
     sides = (bx == 0, bx == nbx - 1, by == 0, by == nby - 1)
     ycol = to_column(sy_ref[...].reshape(1, rows), rows)
     area = ycol * sx_ref[...].reshape(1, lanes)
@@ -271,10 +291,10 @@
         at = pl.ds(pl.multiple_of(z * rows, rows), rows)
         pencil[0, at, k * lanes : (k + 1) * lanes] = value.astype(BF16)
 
-    def ring(phase):
+    def ring(phase, ready=None):
         def hop(number, behind, ahead, s):
             plane = (z - behind + 2 * nz) % nz
-            part = (s + 2 * core) % SUBS
+            part = (s + xl * (SUBS // 2)) % SUBS
             at = pl.ds(pl.multiple_of(plane * rows + part * sub, sub), sub)
             view = pencil.at[phase, at, :]
             return remote(
@@ -290,6 +310,8 @@
 
         parts = range(SUBS)
         for s in parts:
+            if ready is not None:
+                ready(s)
             for number, ahead in enumerate((3, -3)):
                 hop(number, 0, ahead, s).start()
         for s in parts:
@@ -351,41 +373,62 @@
         ]
 
     ring(0)
-    modes_y = contract_y(0)
-
-    for k in range(planes):
-        for side in range(2):
-            tsend[side, k * quarter : (k + 1) * quarter, :] = modes_y[k][
-                side * quarter : (side + 1) * quarter, :
-            ].astype(BF16)
-
-    def t_copy(o):
-        to = (bx + o) % nbx
-        return remote(tsend.at[to % 2], tall.at[bx], t_send.at[o], t_recv.at[o], bx=to)
-
-    def start_t(o, _):
-        t_copy(o).start()
+    shares_x[1].wait_recv()
+    passed = [pass_x(0), pass_x(1)]
+    passed[0].start()
+    shares_y[0].wait_recv()
+    sums = dot(keep_y[0].reshape(2 * rows, keep_y.shape[3]), pencil[0])
+
+    for side in range(2):
+        for r in range(4):
+            for k in range(planes):
+                tsend[side, r, k * quarter : (k + 1) * quarter, :] = sums[
+                    side * rows + r * quarter : side * rows + (r + 1) * quarter,
+                    k * lanes : (k + 1) * lanes,
+                ].astype(BF16)
+
+    def t_copy(t):
+        to, cross = (bx + t) % nbx, t // nbx
+        side = xh + cross - 2 * xh * cross
+        r = 2 * (to // (2 * ny4)) + to % 2
+        return pltpu.make_async_remote_copy(
+            src_ref=tsend.at[side, r],
+            dst_ref=tall.at[xh, bx],
+            send_sem=t_send.at[t],
+            recv_sem=t_recv.at[t],
+            device_id={"bx": to, "by": 2 * z + side},
+            device_id_type=MESH,
+        )
+
+    def start_t(t, _):
+        t_copy(t).start()
         return 0
 
-    lax.fori_loop(1, nbx, start_t, 0)
-    tall[pl.ds(bx, 1)] = tsend[pl.ds(core, 1)]
+    def wait_t(t, _):
+        t_copy(t).wait_recv()
+        return 0
+
+    lax.fori_loop(1, 2 * nbx, start_t, 0)
+    tall[pl.ds(xh, 1), pl.ds(bx, 1)] = tsend[pl.ds(xh, 1), pl.ds(mine4, 1)]
     for load in loads[2:]:
         load.wait()
-    for copy in shares_x:
+    shares_x[3].wait_recv()
+    passed[1].start()
+    for copy in (shares_x[0], shares_x[4], shares_x[5], shares_x[6], passed[0]):
         copy.wait_recv()
-
-    def wait_t(o, _):
-        t_copy(o).wait_recv()
-        return 0
-
-    lax.fori_loop(1, nbx, wait_t, 0)
-    rows_x = jnp.concatenate([tall[n] for n in range(nbx)], axis=1)
-    half_modes = dot_t(rows_x, all_x[0].reshape(2 * lanes, all_x.shape[3]))
-
-    planes_xy = [half_modes[k * quarter : (k + 1) * quarter, :] for k in range(planes)]
-    ey = to_column(ey_ref[...].reshape(1, rows), rows)
-    ey = jnp.where(core == 0, ey[:quarter], ey[quarter:])
-    ex = jnp.concatenate([all_ex[0], all_ex[1]], axis=1)
+    lax.fori_loop(1, 2 * nbx, wait_t, 0)
+    rows_x = jnp.concatenate(
+        [jnp.concatenate([tall[side, n] for n in range(nbx)], axis=1) for side in range(2)], axis=0
+    )
+    both = dot_t(rows_x, all_x[0].reshape(4 * lanes, all_x.shape[3]))
+    part_modes = both[: planes * quarter] + both[planes * quarter :]
+
+    planes_xy = [part_modes[k * quarter : (k + 1) * quarter, :] for k in range(planes)]
+    ey_all = to_column(ey_ref[...].reshape(1, rows), rows)
+    ey = ey_all[:quarter]
+    for r in range(1, 4):
+        ey = jnp.where(mine4 == r, ey_all[r * quarter : (r + 1) * quarter], ey)
+    ex = jnp.concatenate([all_ex[r] for r in range(4)], axis=1)
     fz, iz = fz_ref[...].astype(F32), iz_ref[...].astype(F32)
     scaled = []
     for q in range(planes):
@@ -393,62 +436,72 @@
         scaled.append(mode / (ex + ey + ez_ref[q] + SHIFT))
     for k in range(planes):
         value = sum(iz[k : k + 1, q : q + 1] * scaled[q] for q in range(planes))
-        sall[pl.ds(chip, 1), k * quarter : (k + 1) * quarter, :] = value.astype(BF16)[None]
-
-    def s_copy(o):
-        to = (chip + o) % nchip
-        return remote(
-            sall.at[chip], sall.at[chip], s_send.at[o], s_recv.at[o], bx=to * 2 + core
-        )
-
-    def start_s(o, _):
-        s_copy(o).start()
-        return 0
-
-    def wait_s(o, _):
-        s_copy(o).wait_recv()
-        return 0
-
-    lax.fori_loop(1, nchip, start_s, 0)
-    lax.fori_loop(1, nchip, wait_s, 0)
-    rows_m = jnp.concatenate([sall[n] for n in range(nchip)], axis=1)
-    cells_x = dot_t(rows_m, all_x[1].reshape(2 * lanes, all_x.shape[3])).astype(BF16)
-
-    at = pl.ds(pl.multiple_of(z * rows + core * quarter, quarter), quarter)
-    for k in range(planes):
-        piece = cells_x[k * quarter : (k + 1) * quarter, :]
-        low, high = piece[:, :lanes], piece[:, lanes:]
-        pencil[1, at, k * lanes : (k + 1) * lanes] = jnp.where(core == 0, low, high)
-        uside[:, k * lanes : (k + 1) * lanes] = jnp.where(core == 0, high, low)
-    copy = remote(uside, pencil.at[1, at, :], u_send.at[0], u_recv.at[0], bx=sibling)
-    copy.start()
-    copy.wait()
-
-    ring(1)
+        sall[pl.ds(row4, 1), k * quarter : (k + 1) * quarter, :] = value.astype(BF16)[None]
+
+    s_copies = []
+    for o in range(1, ny4):
+        to = (row4 + o) % ny4
+        at = sall.at[row4]
+        s_copies.append(
+            remote(at, at, s_send.at[o], s_recv.at[o], bx=(xl * ny4 + to) * 2 + core)
+        )
+    for copy in s_copies:
+        copy.start()
+    for copy in (shares_x[2], passed[1]):
+        copy.wait_recv()
+    for copy in s_copies:
+        copy.wait_recv()
+    rows_m = jnp.concatenate(
+        [
+            sall[n, :, (2 * side + c) * lanes : (2 * side + c + 1) * lanes]
+            for side in range(2)
+            for n in range(ny4)
+            for c in range(2)
+        ],
+        axis=1,
+    )
+    cells_x = dot_t(rows_m, all_x[1].reshape(4 * lanes, all_x.shape[3])).astype(BF16)
+
+    at = pl.ds(pl.multiple_of(z * rows + mine4 * quarter, quarter), quarter)
+    for r in range(4):
+        for k in range(planes):
+            uside[r, :, k * lanes : (k + 1) * lanes] = cells_x[
+                k * quarter : (k + 1) * quarter, r * lanes : (r + 1) * lanes
+            ]
+    u_copies = []
+    for j in (2, 3, 1):
+        to, r = relative(j)
+        u_copies.append(
+            remote(uside.at[r], pencil.at[1, at, :], u_send.at[j], u_recv.at[j], bx=to)
+        )
+    for copy in u_copies:
+        copy.start()
+    pencil[1, at, :] = uside[pl.ds(mine4, 1)].reshape(quarter, planes * lanes)
+
+    def ready(s):
+        for copy in u_copies[2:] if s == 0 else u_copies[:2]:
+            copy.wait_recv()
+
+    ring(1, ready)
     field = contract_y(1)
     for k in range(planes):
         out_ref[k] = sol_ref[k] + (sz_ref[k] * area) * field[k]
 
-    for copy in halos + shares_x + shares_y:
+    for copy in halos + shares_x + shares_y + passed + s_copies + u_copies:
         copy.wait_send()
 
-    def end_t(o, _):
-        t_copy(o).wait_send()
+    def end_t(t, _):
+        t_copy(t).wait_send()
         return 0
 
-    def end_s(o, _):
-        s_copy(o).wait_send()
-        return 0
-
-    lax.fori_loop(1, nbx, end_t, 0)
-    lax.fori_loop(1, nchip, end_s, 0)
+    lax.fori_loop(1, 2 * nbx, end_t, 0)
 
 
 def on_device(nbx, nby, *args):
     sol, forward_x = args[0], args[7]
     planes, rows, lanes = sol.shape
     nx, ny = forward_x.shape[1], rows * nby
-    quarter = rows // 2
+    quarter = rows // 4
     wide = planes * lanes
     vmem = pl.BlockSpec(memory_space=pltpu.VMEM)
     far = pl.BlockSpec(memory_space=pltpu.HBM)
@@ -472,32 +525,32 @@
             pltpu.VMEM((2, rows, ny), BF16),
             pltpu.VMEM((2, 2, rows, ny // 2), BF16),
             pltpu.VMEM((2, rows, ny // 2), BF16),
-            pltpu.VMEM((2, 2, lanes, nx), BF16),
-            pltpu.VMEM((2, 1, lanes), F32),
+            pltpu.VMEM((2, 4, lanes, nx), BF16),
+            pltpu.VMEM((4, 1, lanes), F32),
             pltpu.VMEM((2, ny // 2, wide), BF16),
             pltpu.VMEM((2, 2, rows, wide // 2), BF16),
             pltpu.VMEM((2, 2, rows, wide // 2), BF16),
-            pltpu.VMEM((2, planes * quarter, lanes), BF16),
-            pltpu.VMEM((nbx, planes * quarter, lanes), BF16),
-            pltpu.VMEM((nbx // 2, planes * quarter, 2 * lanes), BF16),
-            pltpu.VMEM((quarter, wide), BF16),
+            pltpu.VMEM((2, 4, planes * quarter, lanes), BF16),
+            pltpu.VMEM((2, nbx, planes * quarter, lanes), BF16),
+            pltpu.VMEM((nbx // 4, planes * quarter, 4 * lanes), BF16),
+            pltpu.VMEM((4, quarter, wide), BF16),
             dma((4,)),
             dma((4,)),
             dma((4,)),
             dma((2,)),
             dma((2,)),
-            dma((3,)),
-            dma((3,)),
+            dma((9,)),
+            dma((9,)),
             dma((2, nby // 2 - 1, SUBS)),
             dma((2, nby // 2, SUBS)),
             dma((2, 2)),
             dma((2, 2)),
-            dma((nbx,)),
-            dma((nbx,)),
-            dma((nbx // 2,)),
-            dma((nbx // 2,)),
-            dma((1,)),
-            dma((1,)),
+            dma((2 * nbx,)),
+            dma((2 * nbx,)),
+            dma((nbx // 4,)),
+            dma((nbx // 4,)),
+            dma((4,)),
+            dma((4,)),
         ],
         compiler_params=pltpu.CompilerParams(
             collective_id=0, has_side_effects=True, vmem_limit_bytes=60 << 20

time: 89.3 us -> 89.6 us (level)
  the two profiles are of different devices: /device:TPU:24 before, /device:TPU:1 now
where the time goes in v3:
time: 89.6 us; the launch traced here: 89.4 us
  Pallas kernels  87.8 us (98%)
  local copies, waits for them, and re-layouts  1.57 us (2%)
    pallas_call x1, Pallas kernels, on_device(): pl.pallas_call(functools.partial(kernel, nbx, nby), out_shape=jax.ShapeDt...  87.8 us

profile of v3, /device:TPU:1, one launch (start us, length us, event | category | flops | bytes accessed | tf_op | source)
XLA Modules:
  0.0 89.4 jit_solution(15422622957601194407)
XLA Ops:
  0.0 87.8 %shard_map.154 = f32[4,64,128]{2,1,0:T(8,128)} custom-call(f32[4,64,128]{2,1,0:T(8,128)} %sol_far.1, f32[4,64,128]{2,1,0:T(8,128)} %src_far.1, s32[4,64,128]{2,1,0:T(8,128)} %cls_far.1, f32[8]{0:T(128)} %cond_far.1, f32[128]{0:T(128)} %sx_far.1, f32[64]{0:T(128)} %sy_far.1, f32[4]{0:T(128)} %sz_far.1, bf16[128,2048]{1,0:T(8,128)(2,1)} %fx_ref.1, ...), custom_call_target="tpu_custom_call" | custom-call | tf_op jit(solution)/shard_map/pallas_call | solution.py:511
  87.9 1.6 %copy.18 = f32[4,64,128]{2,1,0:T(8,128)} copy(f32[4,64,128]{2,1,0:T(8,128)} %shard_map.154) | data formatting | bytes 262144

commit v4 on v3

--- a/solution.py
+++ b/solution.py
@@ -43,9 +43,14 @@
     return jnp.where(cn > 0, 2.0 * c * cn / (c + cn), c)
 
 
-def remote(src, dst, send, recv, **where):
+def remote(src, dst, send, recv, bx, by):
     return pltpu.make_async_remote_copy(
-        src_ref=src, dst_ref=dst, send_sem=send, recv_sem=recv, device_id=where, device_id_type=MESH
+        src_ref=src,
+        dst_ref=dst,
+        send_sem=send,
+        recv_sem=recv,
+        device_id={"bx": bx, "by": by},
+        device_id_type=MESH,
     )
 
 
@@ -93,7 +98,8 @@
     pass_y,
     all_x,
     all_ex,
-    pencil,
+    pencil0,
+    pencil1,
     half_out,
     half_in,
     tsend,
@@ -125,32 +131,50 @@
     mine4 = 2 * xl + core
     other = by + 1 - 2 * xh
 
+    chips_x, cores = (xl, 1 - xl), (core, 1 - core)
+    along_y = [2 * row4] + [2 * ((row4 + o) % ny4) for o in range(1, ny4)]
+    starts_x = [value * (2 * ny4) for value in chips_x]
+    sides_y = (by, other)
+
+    def place(dx, dy, dc):
+        return starts_x[dx] + along_y[dy] + cores[dc]
+
     def relative(j):
-        xl2 = xl if j < 2 else 1 - xl
-        core2 = core if j % 2 == 0 else 1 - core
-        return (xl2 * ny4 + row4) * 2 + core2, 2 * xl2 + core2
+        dx, dc = j // 2, j % 2
+        return place(dx, 0, dc), 2 * chips_x[dx] + cores[dc]
+
+    plane_back = {b: (z - b + nz) % nz if b else z for b in (0, 2, -2, 4, -4, 6, -6)}
+    by_ahead = {a: (by + 2 * a + nby) % nby for a in (1, -1, 2, -2, 3, -3)}
+    by_next = ((by + nby - 1) % nby, (by + 1) % nby)
+    bx_next = ((bx + nbx - 1) % nbx, (bx + 1) % nbx)
 
     planes, rows, lanes = sol_ref.shape
     sub = rows // SUBS
     quarter = rows // 4
 
+    part_wide = planes * lanes // SUBS
+    part_planes = planes // SUBS
+    part_rows = part_planes * quarter
     barrier = pltpu.get_barrier_semaphore()
 
-    def greet(o, _):
+    def greet(to_bx, to_by):
         pl.semaphore_signal(
-            barrier, inc=1, device_id={"bx": (bx + o) % nbx}, device_id_type=MESH
+            barrier, inc=1, device_id={"bx": to_bx, "by": to_by}, device_id_type=MESH
         )
-        pl.semaphore_signal(
-            barrier, inc=1, device_id={"bx": (bx + o) % nbx, "by": other}, device_id_type=MESH
-        )
-        return 0
-
-    lax.fori_loop(1, nbx, greet, 0)
-    near = (1, nby - 1, 2, nby - 2, 4, nby - 4, 6, nby - 6)
-    for step in near:
-        pl.semaphore_signal(
-            barrier, inc=1, device_id={"by": (by + step) % nby}, device_id_type=MESH
-        )
+
+    near = (*by_next, *by_ahead.values())
+    for to in near:
+        greet(bx, to)
+    layer = [
+        (dx, dy, dc, cross)
+        for cross in range(2)
+        for dy in range(ny4)
+        for dx in range(2)
+        for dc in range(2)
+    ]
+    for dx, dy, dc, cross in layer:
+        if dx or dy or dc:
+            greet(place(dx, dy, dc), sides_y[cross])
 
     smalls = [
         pltpu.make_async_copy(far, ref, small_sem.at[n])
@@ -203,10 +227,10 @@
     pl.semaphore_wait(barrier, 2 * (nbx - 1) + len(near))
 
     halos = [
-        remote(xmsg.at[0], xhalo.at[1], halo_send.at[0], halo_recv.at[0], bx=(bx + nbx - 1) % nbx),
-        remote(xmsg.at[1], xhalo.at[0], halo_send.at[1], halo_recv.at[1], bx=(bx + 1) % nbx),
-        remote(ymsg.at[0], yhalo.at[1], halo_send.at[2], halo_recv.at[2], by=(by + nby - 1) % nby),
-        remote(ymsg.at[1], yhalo.at[0], halo_send.at[3], halo_recv.at[3], by=(by + 1) % nby),
+        remote(xmsg.at[0], xhalo.at[1], halo_send.at[0], halo_recv.at[0], bx_next[0], by),
+        remote(xmsg.at[1], xhalo.at[0], halo_send.at[1], halo_recv.at[1], bx_next[1], by),
+        remote(ymsg.at[0], yhalo.at[1], halo_send.at[2], halo_recv.at[2], bx, by_next[0]),
+        remote(ymsg.at[1], yhalo.at[0], halo_send.at[3], halo_recv.at[3], bx, by_next[1]),
     ]
     for copy in halos:
         copy.start()
@@ -224,10 +248,26 @@
             keep_y[which, pl.ds(xh, 1), :, where] = jnp.where(xh == 0, zero, one).astype(BF16)[None]
             pass_y[which, :, where] = jnp.where(xh == 0, one, zero).astype(BF16)
         copy = remote(
-            pass_y.at[which], keep_y.at[which, xh], wy_send.at[which], wy_recv.at[which], by=other
+            pass_y.at[which], keep_y.at[which, xh], wy_send.at[which], wy_recv.at[which], bx, other
         )
+        shares_y.append(copy)
+
+    shares_x = []
+    for which, ref in enumerate((fx_ref, ix_ref)):
+        for j in (1, 2):
+            at, number = all_x.at[which, mine4], 3 * which + j - 1
+            shares_x.append(
+                remote(ref, at, wx_send.at[number], wx_recv.at[number], relative(j)[0], by)
+            )
+    for j in (1, 2, 3):
+        at, number = all_ex.at[mine4], 5 + j
+        shares_x.append(remote(at, at, wx_send.at[number], wx_recv.at[number], relative(j)[0], by))
+    for copy in (*shares_x[4:], shares_y[0], shares_x[1], shares_x[0]):
         copy.start()
-        shares_y.append(copy)
+
+    def pass_x(which):
+        at, number = all_x.at[which, relative(2)[1]], 3 * which + 2
+        return remote(at, at, wx_send.at[number], wx_recv.at[number], relative(1)[0], by)
 
     row_at, lane_at = iota((rows, lanes), 0), iota((rows, lanes), 1)
     for k in range(planes):
@@ -248,23 +288,6 @@
         load.wait()
     for copy in halos:
         copy.wait_recv()
-
-    shares_x = []
-    for which, ref in enumerate((fx_ref, ix_ref)):
-        for j in (1, 2):
-            at, number = all_x.at[which, mine4], 3 * which + j - 1
-            shares_x.append(
-                remote(ref, at, wx_send.at[number], wx_recv.at[number], bx=relative(j)[0])
-            )
-    for j in (1, 2, 3):
-        at, number = all_ex.at[mine4], 5 + j
-        shares_x.append(remote(at, at, wx_send.at[number], wx_recv.at[number], bx=relative(j)[0]))
-    for copy in shares_x[4:] + shares_x[:4]:
-        copy.start()
-
-    def pass_x(which):
-        at, number = all_x.at[which, relative(2)[1]], 3 * which + 2
-        return remote(at, at, wx_send.at[number], wx_recv.at[number], bx=relative(1)[0])
 
     sides = (bx == 0, bx == nbx - 1, by == 0, by == nby - 1)
     ycol = to_column(sy_ref[...].reshape(1, rows), rows)
@@ -289,67 +312,75 @@
             total = total + jnp.where(row_at == edge, term, 0.0)
         value = (sz_ref[k] * area) * (src_ref[k] - total)
         at = pl.ds(pl.multiple_of(z * rows, rows), rows)
-        pencil[0, at, k * lanes : (k + 1) * lanes] = value.astype(BF16)
-
-    def ring(phase, ready=None):
+        at2 = (k % part_planes) * lanes
+        pencil0[k // part_planes, at, at2 : at2 + lanes] = value.astype(BF16)
+
+    ended = []
+
+    def ring(phase, ready=None, done=None):
         def hop(number, behind, ahead, s):
-            plane = (z - behind + 2 * nz) % nz
-            part = (s + xl * (SUBS // 2)) % SUBS
-            at = pl.ds(pl.multiple_of(plane * rows + part * sub, sub), sub)
-            view = pencil.at[phase, at, :]
+            plane = plane_back[behind]
+            if phase == 0:
+                view = pencil0.at[s, pl.ds(pl.multiple_of(plane * rows, rows), rows)]
+            else:
+                part = (s + xl * (SUBS // 2)) % SUBS
+                view = pencil1.at[pl.ds(pl.multiple_of(plane * rows + part * sub, sub), sub)]
             return remote(
                 view,
                 view,
                 ring_send.at[phase, number, s],
                 ring_recv.at[phase, (behind + ahead) % nz, s],
-                by=(by + 2 * ahead + nby) % nby,
+                bx,
+                by_ahead[ahead],
             )
 
         def arrive(behind, s):
-            hop(0, behind, 0, s).wait_recv()
+            view = pencil1.at[pl.ds(0, sub), :]
+            send, recv = ring_send.at[phase, 0, s], ring_recv.at[phase, behind % nz, s]
+            remote(view, view, send, recv, bx, other).wait_recv()
 
         parts = range(SUBS)
         for s in parts:
             if ready is not None:
                 ready(s)
-            for number, ahead in enumerate((3, -3)):
+            for number, ahead in enumerate((2, -2)):
                 hop(number, 0, ahead, s).start()
         for s in parts:
             for number, ahead in enumerate((1, -1)):
                 hop(2 + number, 0, ahead, s).start()
-        for s in parts:
-            for side, sign in enumerate((1, -1)):
-                arrive(3 * sign, s)
-                for number, ahead in enumerate((3 * sign, sign, -sign)):
-                    hop(4 + 3 * side + number, 3 * sign, ahead, s).start()
+        for stage, far in enumerate((2, 4)):
+            for s in parts:
+                for side, sign in enumerate((1, -1)):
+                    arrive(far * sign, s)
+                    for number, ahead in enumerate((2 * sign, sign)):
+                        hop(4 + 4 * stage + 2 * side + number, far * sign, ahead, s).start()
         for s in parts:
             for side, sign in enumerate((1, -1)):
                 arrive(6 * sign, s)
-                for number, ahead in enumerate((sign, -sign)):
-                    hop(10 + 2 * side + number, 6 * sign, ahead, s).start()
+                hop(12 + side, 6 * sign, sign, s).start()
                 if (s < SUBS // 2) == (side == 0):
                     hop(14, 6 * sign, 2 * sign, s).start()
-        for behind in (1, 2, 4, 5, 7):
-            for s in parts:
+        for s in parts:
+            for behind in (1, 3, 5, 7):
                 for sign in (1, -1):
                     arrive(behind * sign, s)
-        for s in parts:
             arrive(8, s)
-
-        def finish(number, _):
+            if done is not None:
+                done(s)
+
+        for number in range(nz - 1):
             for s in parts:
-                hop(number, 0, 1, s).wait_send()
-            return 0
-
-        lax.fori_loop(0, 15, finish, 0)
+                view = pencil1.at[pl.ds(0, sub), :]
+                send, recv = ring_send.at[phase, number, s], ring_recv.at[phase, 0, s]
+                ended.append(remote(view, view, send, recv, bx, other))
 
     def contract_y(phase):
         shares_y[phase].wait_recv()
-        width = pencil.shape[2] // 2
+        width = pencil1.shape[1] // 2
         mine, copies = [], []
         for piece in range(2):
             at = slice(piece * width, (piece + 1) * width)
-            whole = pencil[phase, :, at]
+            whole = pencil1[:, at]
             gone = dot(keep_y[phase, 1 - xh], whole)
             half_out[phase, piece] = gone.astype(BF16)
             copy = remote(
@@ -357,7 +388,8 @@
                 half_in.at[phase, piece],
                 half_send.at[phase, piece],
                 half_recv.at[phase, piece],
-                by=other,
+                bx,
+                other,
             )
             copy.start()
             copies.append(copy)
@@ -372,53 +404,59 @@
             for k in range(planes)
         ]
 
-    ring(0)
-    shares_x[1].wait_recv()
+    xh_of = (xh, 1 - xh)
+    t_copies = []
     passed = [pass_x(0), pass_x(1)]
-    passed[0].start()
-    shares_y[0].wait_recv()
-    sums = dot(keep_y[0].reshape(2 * rows, keep_y.shape[3]), pencil[0])
-
-    for side in range(2):
-        for r in range(4):
-            for k in range(planes):
-                tsend[side, r, k * quarter : (k + 1) * quarter, :] = sums[
-                    side * rows + r * quarter : side * rows + (r + 1) * quarter,
-                    k * lanes : (k + 1) * lanes,
-                ].astype(BF16)
-
-    def t_copy(t):
-        to, cross = (bx + t) % nbx, t // nbx
-        side = xh + cross - 2 * xh * cross
-        r = 2 * (to // (2 * ny4)) + to % 2
-        return pltpu.make_async_remote_copy(
-            src_ref=tsend.at[side, r],
-            dst_ref=tall.at[xh, bx],
-            send_sem=t_send.at[t],
-            recv_sem=t_recv.at[t],
-            device_id={"bx": to, "by": 2 * z + side},
-            device_id_type=MESH,
-        )
-
-    def start_t(t, _):
-        t_copy(t).start()
-        return 0
-
-    def wait_t(t, _):
-        t_copy(t).wait_recv()
-        return 0
-
-    lax.fori_loop(1, 2 * nbx, start_t, 0)
-    tall[pl.ds(xh, 1), pl.ds(bx, 1)] = tsend[pl.ds(xh, 1), pl.ds(mine4, 1)]
+
+    def send_part(s):
+        if s == 0:
+            shares_y[0].wait_recv()
+            shares_x[1].wait_recv()
+            passed[0].start()
+        sums = dot(keep_y[0].reshape(2 * rows, keep_y.shape[3]), pencil0[s]).astype(BF16)
+        for side in range(2):
+            for r in range(4):
+                for k in range(part_planes):
+                    row = side * rows + r * quarter
+                    tsend[s, side, r, k * quarter : (k + 1) * quarter, :] = sums[
+                        row : row + quarter, k * lanes : (k + 1) * lanes
+                    ]
+        for t, (dx, dy, dc, cross) in enumerate(layer):
+            if t:
+                copy = remote(
+                    tsend.at[s, xh_of[cross], 2 * chips_x[dx] + cores[dc]],
+                    tall.at[s, xh, bx],
+                    t_send.at[t, s],
+                    t_recv.at[((-dy) % ny4 * 4 + t % 4) + t // (4 * ny4) * (4 * ny4), s],
+                    place(dx, dy, dc),
+                    sides_y[cross],
+                )
+                copy.start()
+                t_copies.append(copy)
+        tall[s, pl.ds(xh, 1), pl.ds(bx, 1)] = tsend[s, pl.ds(xh, 1), pl.ds(mine4, 1)]
+
+    ring(0, done=send_part)
+    for copy in (shares_x[3], shares_x[2]):
+        copy.start()
+
+    def wait_t():
+        for t in range(1, len(layer)):
+            for s in range(SUBS):
+                at = tall.at[0, 0, 0]
+                remote(at, at, t_send.at[t, s], t_recv.at[t, s], bx, other).wait_recv()
+
     for load in loads[2:]:
         load.wait()
-    shares_x[3].wait_recv()
-    passed[1].start()
     for copy in (shares_x[0], shares_x[4], shares_x[5], shares_x[6], passed[0]):
         copy.wait_recv()
-    lax.fori_loop(1, 2 * nbx, wait_t, 0)
+    wait_t()
     rows_x = jnp.concatenate(
-        [jnp.concatenate([tall[side, n] for n in range(nbx)], axis=1) for side in range(2)], axis=0
+        [
+            jnp.concatenate([tall[s, side, n] for n in range(nbx)], axis=1)
+            for side in range(2)
+            for s in range(SUBS)
+        ],
+        axis=0,
     )
     both = dot_t(rows_x, all_x[0].reshape(4 * lanes, all_x.shape[3]))
     part_modes = both[: planes * quarter] + both[planes * quarter :]
@@ -440,13 +478,12 @@
 
     s_copies = []
     for o in range(1, ny4):
-        to = (row4 + o) % ny4
         at = sall.at[row4]
-        s_copies.append(
-            remote(at, at, s_send.at[o], s_recv.at[o], bx=(xl * ny4 + to) * 2 + core)
-        )
+        s_copies.append(remote(at, at, s_send.at[o], s_recv.at[o], place(0, o, 0), by))
     for copy in s_copies:
         copy.start()
+    shares_x[3].wait_recv()
+    passed[1].start()
     for copy in (shares_x[2], passed[1]):
         copy.wait_recv()
     for copy in s_copies:
@@ -472,11 +509,12 @@
     for j in (2, 3, 1):
         to, r = relative(j)
         u_copies.append(
-            remote(uside.at[r], pencil.at[1, at, :], u_send.at[j], u_recv.at[j], bx=to)
+            remote(uside.at[r], pencil1.at[at, :], u_send.at[j], u_recv.at[j], to, by)
         )
     for copy in u_copies:
         copy.start()
-    pencil[1, at, :] = uside[pl.ds(mine4, 1)].reshape(quarter, planes * lanes)
+    shares_y[1].start()
+    pencil1[at, :] = uside[pl.ds(mine4, 1)].reshape(quarter, planes * lanes)
 
     def ready(s):
         for copy in u_copies[2:] if s == 0 else u_copies[:2]:
@@ -487,14 +525,8 @@
     for k in range(planes):
         out_ref[k] = sol_ref[k] + (sz_ref[k] * area) * field[k]
 
-    for copy in halos + shares_x + shares_y + passed + s_copies + u_copies:
+    for copy in halos + shares_x + shares_y + passed + s_copies + u_copies + t_copies + ended:
         copy.wait_send()
-
-    def end_t(t, _):
-        t_copy(t).wait_send()
-        return 0
-
-    lax.fori_loop(1, 2 * nbx, end_t, 0)
 
 
 def on_device(nbx, nby, *args):
@@ -527,11 +559,12 @@
             pltpu.VMEM((2, rows, ny // 2), BF16),
             pltpu.VMEM((2, 4, lanes, nx), BF16),
             pltpu.VMEM((4, 1, lanes), F32),
-            pltpu.VMEM((2, ny // 2, wide), BF16),
+            pltpu.VMEM((SUBS, ny // 2, wide // SUBS), BF16),
+            pltpu.VMEM((ny // 2, wide), BF16),
             pltpu.VMEM((2, 2, rows, wide // 2), BF16),
             pltpu.VMEM((2, 2, rows, wide // 2), BF16),
-            pltpu.VMEM((2, 4, planes * quarter, lanes), BF16),
-            pltpu.VMEM((2, nbx, planes * quarter, lanes), BF16),
+            pltpu.VMEM((SUBS, 2, 4, planes * quarter // SUBS, lanes), BF16),
+            pltpu.VMEM((SUBS, 2, nbx, planes * quarter // SUBS, lanes), BF16),
             pltpu.VMEM((nbx // 4, planes * quarter, 4 * lanes), BF16),
             pltpu.VMEM((4, quarter, wide), BF16),
             dma((4,)),
@@ -545,8 +578,8 @@
             dma((2, nby // 2, SUBS)),
             dma((2, 2)),
             dma((2, 2)),
-            dma((2 * nbx,)),
-            dma((2 * nbx,)),
+            dma((2 * nbx, SUBS)),
+            dma((2 * nbx, SUBS)),
             dma((nbx // 4,)),
             dma((nbx // 4,)),
             dma((4,)),

time: 89.6 us -> 85.6 us (0.955)
  the two profiles are of different devices: /device:TPU:1 before, /device:TPU:24 now
where the time goes in v4:
time: 85.6 us; the launch traced here: 84.9 us
  Pallas kernels  83.3 us (97%)
  local copies, waits for them, and re-layouts  1.57 us (2%)
    pallas_call x1, Pallas kernels, on_device(): pl.pallas_call(functools.partial(kernel, nbx, nby), out_shape=jax.ShapeDt...  83.3 us

profile of v4, /device:TPU:24, one launch (start us, length us, event | category | flops | bytes accessed | tf_op | source)
XLA Modules:
  0.0 84.9 jit_solution(8852055661948820959)
XLA Ops:
  0.0 83.3 %shard_map.154 = f32[4,64,128]{2,1,0:T(8,128)} custom-call(f32[4,64,128]{2,1,0:T(8,128)} %sol_far.1, f32[4,64,128]{2,1,0:T(8,128)} %src_far.1, s32[4,64,128]{2,1,0:T(8,128)} %cls_far.1, f32[8]{0:T(128)} %cond_far.1, f32[128]{0:T(128)} %sx_far.1, f32[64]{0:T(128)} %sy_far.1, f32[4]{0:T(128)} %sz_far.1, bf16[128,2048]{1,0:T(8,128)(2,1)} %fx_ref.1, ...), custom_call_target="tpu_custom_call" | custom-call | tf_op jit(solution)/shard_map/pallas_call | solution.py:543
  83.3 1.6 %copy.18 = f32[4,64,128]{2,1,0:T(8,128)} copy(f32[4,64,128]{2,1,0:T(8,128)} %shard_map.154) | data formatting | bytes 262144

commit v5 on v4

--- a/solution.py
+++ b/solution.py
@@ -237,7 +237,8 @@
 
     shares_y = []
     low_lane = iota((rows, 128), 1) < 64
-    for which in range(2):
+
+    def compact(which):
         loads[which].wait()
         for pair in range(raw_y.shape[2] // 256):
             a = raw_y[which, :, 256 * pair : 256 * pair + 128].astype(F32)
@@ -251,6 +252,8 @@
             pass_y.at[which], keep_y.at[which, xh], wy_send.at[which], wy_recv.at[which], bx, other
         )
         shares_y.append(copy)
+
+    compact(0)
 
     shares_x = []
     for which, ref in enumerate((fx_ref, ix_ref)):
@@ -438,6 +441,7 @@
     ring(0, done=send_part)
     for copy in (shares_x[3], shares_x[2]):
         copy.start()
+    compact(1)
 
     def wait_t():
         for t in range(1, len(layer)):

time: 85.6 us -> 85.4 us (level)
  no operation moved by 1% of the time
where the time goes in v5:
time: 85.4 us; the launch traced here: 85.3 us
  Pallas kernels  83.7 us (98%)
  local copies, waits for them, and re-layouts  1.57 us (2%)
    pallas_call x1, Pallas kernels, on_device(): pl.pallas_call(functools.partial(kernel, nbx, nby), out_shape=jax.ShapeDt...  83.7 us

profile of v5, /device:TPU:24, one launch (start us, length us, event | category | flops | bytes accessed | tf_op | source)
XLA Modules:
  0.0 85.3 jit_solution(4063845294154732265)
XLA Ops:
  0.0 83.7 %shard_map.154 = f32[4,64,128]{2,1,0:T(8,128)} custom-call(f32[4,64,128]{2,1,0:T(8,128)} %sol_far.1, f32[4,64,128]{2,1,0:T(8,128)} %src_far.1, s32[4,64,128]{2,1,0:T(8,128)} %cls_far.1, f32[8]{0:T(128)} %cond_far.1, f32[128]{0:T(128)} %sx_far.1, f32[64]{0:T(128)} %sy_far.1, f32[4]{0:T(128)} %sz_far.1, bf16[128,2048]{1,0:T(8,128)(2,1)} %fx_ref.1, ...), custom_call_target="tpu_custom_call" | custom-call | tf_op jit(solution)/shard_map/pallas_call | solution.py:547
  83.7 1.6 %copy.18 = f32[4,64,128]{2,1,0:T(8,128)} copy(f32[4,64,128]{2,1,0:T(8,128)} %shard_map.154) | data formatting | bytes 262144

commit v6 on v5

--- a/solution.py
+++ b/solution.py
@@ -396,7 +396,9 @@
             )
             copy.start()
             copies.append(copy)
-            mine.append(dot(keep_y[phase, xh], whole))
+        for piece in range(2):
+            at = slice(piece * width, (piece + 1) * width)
+            mine.append(dot(keep_y[phase, xh], pencil1[:, at]))
         for piece in range(2):
             copies[piece].wait_recv()
             mine[piece] = mine[piece] + half_in[phase, piece].astype(F32)

time: 85.4 us -> 85.4 us (level)
  no operation moved by 1% of the time
where the time goes in v6:
time: 85.4 us; the launch traced here: 85.3 us
  Pallas kernels  83.7 us (98%)
  local copies, waits for them, and re-layouts  1.57 us (2%)
    pallas_call x1, Pallas kernels, on_device(): pl.pallas_call(functools.partial(kernel, nbx, nby), out_shape=jax.ShapeDt...  83.7 us

profile of v6, /device:TPU:24, one launch (start us, length us, event | category | flops | bytes accessed | tf_op | source)
XLA Modules:
  0.0 85.3 jit_solution(908613313142203377)
XLA Ops:
  0.0 83.7 %shard_map.154 = f32[4,64,128]{2,1,0:T(8,128)} custom-call(f32[4,64,128]{2,1,0:T(8,128)} %sol_far.1, f32[4,64,128]{2,1,0:T(8,128)} %src_far.1, s32[4,64,128]{2,1,0:T(8,128)} %cls_far.1, f32[8]{0:T(128)} %cond_far.1, f32[128]{0:T(128)} %sx_far.1, f32[64]{0:T(128)} %sy_far.1, f32[4]{0:T(128)} %sz_far.1, bf16[128,2048]{1,0:T(8,128)(2,1)} %fx_ref.1, ...), custom_call_target="tpu_custom_call" | custom-call | tf_op jit(solution)/shard_map/pallas_call | solution.py:549
  83.7 1.6 %copy.18 = f32[4,64,128]{2,1,0:T(8,128)} copy(f32[4,64,128]{2,1,0:T(8,128)} %shard_map.154) | data formatting | bytes 262144
